TPU v7x, 32 devices: a whole 2x2x4 slice. The times are simulated.
32 devices in a mesh: dp: 4 (over y, core), seq: 8 (over z, x).
Axes of the slice: x: 2, y: 2, z: 4, core: 2. Of those that a mesh axis runs over, the one named last changes fastest.
Arguments:
- patches: bfloat16 [8192, 768], P(('dp', 'seq')), may hold values from -6 to 6
- cotangent: bfloat16 [8192, 768], P(('dp', 'seq')), may hold values from -6 to 6
- input_views: int32 [4], P('dp'), may hold values from 1 to 1, as said below
- token_live: int32 [8192], P(('dp', 'seq')), may hold values from 0 to 1, as said below
- master: float32 [768, 12, 768], P('dp', None, 'seq')
- moment_one: float32 [768, 12, 768], P('dp', None, 'seq')
- moment_two: float32 [768, 12, 768], P('dp', None, 'seq'), as said below
- norm_params: float32 [4, 768], replicated, as said below
- norm_moment_one: float32 [4, 768], replicated
- norm_moment_two: float32 [4, 768], replicated, as said below
Outputs:
- block_out: bfloat16 [8192, 768], P(('dp', 'seq'))
- patches_grad: float32 [8192, 768], P(('dp', 'seq'))
- new_master: float32 [768, 12, 768], P('dp', None, 'seq')
- new_copy: bfloat16 [768, 12, 768], P('dp', None, 'seq')
- new_moment_one: float32 [768, 12, 768], P('dp', None, 'seq')
- new_moment_two: float32 [768, 12, 768], P('dp', None, 'seq')
- new_norm_params: float32 [4, 768], replicated
- new_norm_moment_one: float32 [4, 768], replicated
- new_norm_moment_two: float32 [4, 768], replicated
- grad_norm: float32 [], replicated
Inputs may be any that keep to these rules, and one draw needn't show every extreme that they name: Scene g's first input_views[g] views are input views, the rest target views. `token_live`: the first patch of every view is present. `moment_two`: positive. `norm_params`: rows 0 and 2 are positive. `norm_moment_two`: positive.
All inputs are finite; a program needn't handle non-finite values.
Results may differ from a plain program's by a relative error of at most 0.017.
Values may be sent and summed in bfloat16 or wider, within the bound.
No kernel may reach another device: no remote copies, remote signals or barrier semaphores. Data moves between devices by JAX's collectives and lax.ppermute only.
A program may use at most 192 MiB of HBM per device.

v0:
```python
from functools import partial
import math

import jax
import jax.numpy as jnp
from jax import lax
from jax.sharding import PartitionSpec as P

D = 768
HEADS = 12
HEAD_DIM = 64
FF = 3072
VIEW = 1024
STEP = 10


layer_eps = 1e-05
beta_first = 0.9
beta_second = 0.95
adam_eps = 1e-08
rate_matrix = 0.08
rate_vector = 0.8
weight_decay = 0.1
masked_score = -1e30


def shifted_2(x, axis, by):
    count = lax.axis_size(axis)
    return lax.ppermute(x, axis, [(i, (i + by) % count) for i in range(count)])


def layer_stats(values):
    centre = jnp.mean(values, axis=-1, keepdims=True)
    shifted = values - centre
    spread = jnp.mean(shifted * shifted, axis=-1, keepdims=True)
    inverse = lax.rsqrt(spread + layer_eps)
    return (shifted * inverse, inverse)


def layer_back(grad_normed, normalized, inverse, gain):
    scaled = grad_normed * gain
    centred = jnp.mean(scaled, axis=-1, keepdims=True)
    along = jnp.mean(scaled * normalized, axis=-1, keepdims=True)
    return inverse * (scaled - centred - normalized * along)


def full_rows(blocks):
    return lax.all_gather(blocks, "dp", axis=0, tiled=True)


def spread_blocks(activation, blocks):
    gathered = full_rows(blocks)
    return jnp.einsum(
        "td,dbc->tbc",
        activation,
        lax.all_gather(gathered, "seq", axis=2, tiled=True),
        preferred_element_type=jnp.float32,
    )


def collect_blocks(grads, blocks):
    gathered = full_rows(blocks)
    initial = jnp.zeros((grads.shape[0], gathered.shape[0]), jnp.float32)
    pieces = lax.all_gather(gathered, "seq", axis=2, tiled=True)
    columns = lax.slice_in_dim(grads, 0, pieces.shape[2], axis=2)
    return initial + jnp.einsum("tbc,dbc->td", columns, pieces, preferred_element_type=jnp.float32)


def reduce_grads(left, right):
    row_share = lax.psum_scatter(
        jnp.einsum("td,tbc->dbc", left, right, preferred_element_type=jnp.float32).astype(
            jnp.bfloat16
        ),
        "dp",
        scatter_dimension=0,
        tiled=True,
    )
    return lax.psum_scatter(row_share, "seq", scatter_dimension=2, tiled=True).astype(jnp.float32)


def split_heads(matrix):
    return matrix.reshape(matrix.shape[0], HEADS, HEAD_DIM)


def visibility(query_view, key_view, key_live, inputs_seen):
    return (key_live[None, :] > 0) & (
        (key_view[None, :] < inputs_seen) | (key_view[None, :] == query_view[:, None])
    )


def attend_forward(query_rows, key_rows, value_rows, living, query_view, inputs_seen):
    tokens = query_rows.shape[0]
    scaling = 1.0 / math.sqrt(HEAD_DIM)
    query_heads = split_heads(query_rows)
    running_max = jnp.full((HEADS, tokens), masked_score, jnp.float32)
    keys_here = lax.all_gather(key_rows, "seq", axis=0, tiled=True)
    values_here = lax.all_gather(value_rows, "seq", axis=0, tiled=True)
    live_here = lax.all_gather(living, "seq", axis=0, tiled=True)
    number = keys_here.shape[0]
    key_view = jnp.arange(number, dtype=jnp.int32) // VIEW
    visible = visibility(query_view, key_view, live_here, inputs_seen)[None]
    scores = (
        jnp.einsum(
            "qhd,khd->hqk", query_heads, split_heads(keys_here), preferred_element_type=jnp.float32
        )
        * scaling
    )
    scores = jnp.where(visible, scores, masked_score)
    new_max = jnp.maximum(running_max, jnp.max(scores, axis=-1))
    weights_now = jnp.where(visible, jnp.exp(scores - new_max[:, :, None]), 0.0)
    summed = jnp.sum(weights_now, axis=-1)
    update = jnp.einsum(
        "hqk,khd->hqd",
        weights_now.astype(jnp.bfloat16),
        split_heads(values_here),
        preferred_element_type=jnp.float32,
    )
    running_max, summed, weighted = (new_max, summed, update)
    output = weighted / summed[:, :, None]
    logsum = running_max + jnp.log(summed)
    return (jnp.transpose(output, (1, 0, 2)).reshape(tokens, HEADS * HEAD_DIM), logsum)


def attend_back(
    query_heads,
    grad_heads,
    logsum,
    delta,
    query_view,
    key_rows,
    value_rows,
    key_live,
    key_offset,
    inputs_seen,
):
    scaling = 1.0 / math.sqrt(HEAD_DIM)
    number = key_rows.shape[0]
    key_view = (key_offset + jnp.arange(number, dtype=jnp.int32)) // VIEW
    visible = visibility(query_view, key_view, key_live, inputs_seen)[None]
    key_heads = split_heads(key_rows)
    value_heads = split_heads(value_rows)
    scores = (
        jnp.einsum("qhd,khd->hqk", query_heads, key_heads, preferred_element_type=jnp.float32)
        * scaling
    )
    weights_now = jnp.where(visible, jnp.exp(scores - logsum[:, :, None]), 0.0)
    grad_weights = jnp.einsum(
        "qhd,khd->hqk", grad_heads, value_heads, preferred_element_type=jnp.float32
    )
    grad_scores = (weights_now * (grad_weights - delta[:, :, None])).astype(jnp.bfloat16)
    query_term = (
        jnp.einsum("hqk,khd->qhd", grad_scores, key_heads, preferred_element_type=jnp.float32)
        * scaling
    )
    key_term = (
        jnp.einsum("hqk,qhd->khd", grad_scores, query_heads, preferred_element_type=jnp.float32)
        * scaling
    )
    value_term = jnp.einsum(
        "hqk,qhd->khd",
        weights_now.astype(jnp.bfloat16),
        grad_heads,
        preferred_element_type=jnp.float32,
    )
    width = HEADS * HEAD_DIM
    return (
        query_term.reshape(-1, width),
        key_term.reshape(number, width),
        value_term.reshape(number, width),
    )


def adam_step(params, grads, first, second, rate, decay):
    first_new = beta_first * first + (1.0 - beta_first) * grads
    second_new = beta_second * second + (1.0 - beta_second) * grads * grads
    first_hat = first_new / (1.0 - beta_first**STEP)
    second_hat = second_new / (1.0 - beta_second**STEP)
    params_new = params - rate * (first_hat / (jnp.sqrt(second_hat) + adam_eps) + decay * params)
    return (params_new, first_new, second_new)


def local(
    patches,
    cotangent,
    input_views,
    token_live,
    master,
    moment_one,
    moment_two,
    norm_params,
    norm_moment_one,
    norm_moment_two,
):
    tokens = patches.shape[0]
    wide_blocks = FF // D
    first_down = 4 + wide_blocks
    seq_count = lax.axis_size("seq")
    seq_index = lax.axis_index("seq")
    inputs_seen = input_views[0]
    positions = jnp.arange(tokens, dtype=jnp.int32)
    own_view = (seq_index * tokens + positions) // VIEW
    copy_low = master.astype(jnp.bfloat16)
    gain_one = norm_params[0]
    shift_one = norm_params[1]
    gain_two = norm_params[2]
    shift_two = norm_params[3]
    patch_float = patches.astype(jnp.float32)
    normal_one, inverse_one = layer_stats(patch_float)
    act_one = (normal_one * gain_one + shift_one).astype(jnp.bfloat16)
    projected = spread_blocks(act_one, copy_low[:, 0:3, :]).astype(jnp.bfloat16)
    query_rows = projected[:, 0, :]
    key_rows = projected[:, 1, :]
    value_rows = projected[:, 2, :]
    living = token_live.astype(jnp.bfloat16)
    attended, logsum = attend_forward(
        query_rows, key_rows, value_rows, living, own_view, inputs_seen
    )
    act_two = attended.astype(jnp.bfloat16)
    branch_one = spread_blocks(act_two, copy_low[:, 3:4, :])[:, 0, :]
    resid = patch_float + branch_one
    normal_two, inverse_two = layer_stats(resid)
    act_three = (normal_two * gain_two + shift_two).astype(jnp.bfloat16)
    widened = spread_blocks(act_three, copy_low[:, 4:first_down, :])
    activated, gelu_pull = jax.vjp(partial(jax.nn.gelu, approximate=False), widened)
    hidden = activated.astype(jnp.bfloat16)
    branch_two = collect_blocks(hidden, copy_low[:, first_down:, :])
    block_out = (resid + branch_two).astype(jnp.bfloat16)
    grad_down = reduce_grads(cotangent, hidden)
    grad_hidden = spread_blocks(cotangent, copy_low[:, first_down:, :])
    grad_wide = gelu_pull(grad_hidden)[0].astype(jnp.bfloat16)
    grad_up = reduce_grads(act_three, grad_wide)
    grad_three = collect_blocks(grad_wide, copy_low[:, 4:first_down, :])
    gain_two_grad = jnp.sum(grad_three * normal_two, axis=0)
    shift_two_grad = jnp.sum(grad_three, axis=0)
    grad_resid = cotangent.astype(jnp.float32) + layer_back(
        grad_three, normal_two, inverse_two, gain_two
    )
    grad_branch = grad_resid.astype(jnp.bfloat16)[:, None, :]
    grad_out_proj = reduce_grads(act_two, grad_branch)
    grad_attended = collect_blocks(grad_branch, copy_low[:, 3:4, :]).astype(jnp.bfloat16)
    grad_heads = split_heads(grad_attended)
    delta = jnp.transpose(jnp.sum(grad_heads.astype(jnp.float32) * split_heads(attended), axis=-1))
    query_heads = split_heads(query_rows)
    zero_rows = jnp.zeros((tokens, HEADS * HEAD_DIM), jnp.float32)

    def pass_key_grads(key_grad, value_grad):
        return (
            shifted_2(key_grad.astype(jnp.bfloat16), "seq", 1).astype(key_grad.dtype),
            shifted_2(value_grad.astype(jnp.bfloat16), "seq", 1).astype(value_grad.dtype),
        )

    def key_turn(turn_index, running):
        keys_now, values_now, live_now, key_grad, value_grad, query_grad = running
        source = (seq_index - turn_index) % seq_count
        query_term, key_term, value_term = attend_back(
            query_heads,
            grad_heads,
            logsum,
            delta,
            own_view,
            keys_now,
            values_now,
            live_now,
            source * tokens,
            inputs_seen,
        )
        keys_next, values_next, live_next = shifted_2((keys_now, values_now, live_now), "seq", 1)
        key_next, value_next = pass_key_grads(key_grad + key_term, value_grad + value_term)
        return (keys_next, values_next, live_next, key_next, value_next, query_grad + query_term)

    cycle_state = lax.fori_loop(
        0, seq_count - 1, key_turn, (key_rows, value_rows, living, zero_rows, zero_rows, zero_rows)
    )
    keys_now, values_now, live_now, key_grad, value_grad, query_grad = cycle_state
    source = (seq_index - (seq_count - 1)) % seq_count
    query_term, key_term, value_term = attend_back(
        query_heads,
        grad_heads,
        logsum,
        delta,
        own_view,
        keys_now,
        values_now,
        live_now,
        source * tokens,
        inputs_seen,
    )
    key_grad, value_grad = pass_key_grads(key_grad + key_term, value_grad + value_term)
    query_grad = query_grad + query_term
    grad_qkv = jnp.stack([query_grad, key_grad, value_grad], axis=1).astype(jnp.bfloat16)
    grad_in_proj = reduce_grads(act_one, grad_qkv)
    grad_one = collect_blocks(grad_qkv, copy_low[:, 0:3, :])
    gain_one_grad = jnp.sum(grad_one * normal_one, axis=0)
    shift_one_grad = jnp.sum(grad_one, axis=0)
    patches_grad = grad_resid + layer_back(grad_one, normal_one, inverse_one, gain_one)
    weight_grad = jnp.concatenate([grad_in_proj, grad_out_proj, grad_up, grad_down], axis=1)
    param_grad = lax.psum(
        jnp.stack([gain_one_grad, shift_one_grad, gain_two_grad, shift_two_grad]), ("dp", "seq")
    )
    device_count = lax.axis_size("dp") * seq_count
    squares = jnp.sum(weight_grad * weight_grad) + jnp.sum(param_grad * param_grad) / device_count
    grad_norm = jnp.sqrt(lax.psum(squares, ("dp", "seq")))
    clip = 1.0 / jnp.maximum(grad_norm, 1.0)
    new_master, new_moment_one, new_moment_two = adam_step(
        master, weight_grad * clip, moment_one, moment_two, rate_matrix, weight_decay
    )
    new_norm_params, new_norm_moment_one, new_norm_moment_two = adam_step(
        norm_params, param_grad * clip, norm_moment_one, norm_moment_two, rate_vector, 0.0
    )
    return (
        block_out,
        patches_grad,
        new_master,
        new_master.astype(jnp.bfloat16),
        new_moment_one,
        new_moment_two,
        new_norm_params,
        new_norm_moment_one,
        new_norm_moment_two,
        grad_norm,
    )


def solution(mesh):
    placed = (
        P(("dp", "seq"), None),
        P(("dp", "seq"), None),
        P("dp"),
        P(("dp", "seq")),
        P("dp", None, "seq"),
        P("dp", None, "seq"),
        P("dp", None, "seq"),
        P(),
        P(),
        P(),
    )
    return jax.shard_map(
        local,
        mesh=mesh,
        in_specs=placed,
        out_specs=(
            P(("dp", "seq"), None),
            P(("dp", "seq"), None),
            P("dp", None, "seq"),
            P("dp", None, "seq"),
            P("dp", None, "seq"),
            P("dp", None, "seq"),
            P(),
            P(),
            P(),
            P(),
        ),
        check_vma=False,
    )
```

profile of v0, /device:TPU:0, one launch (start us, length us, event | category | flops | bytes accessed | tf_op | source)
XLA Modules:
  0.0 1216.7 jit_solution(2378165974198870254)
XLA Ops:
  9.3 10.1 all_gather.42
  21.7 65.1 %all-gather.10.cloned.1.call-done = bf16[768,3,768]{0,2,1:T(8,128)(2,1)} async-done(((bf16[768,3,96]{0,2,1:T(8,128)(2,1)}), bf16[768,3,768]{0,2,1:T(8,128)(2,1)}) %all-gather.10.cloned.1.call-update) | async-done | bytes 3538960 | tf_op jit(solution)/shard_map/all_gather | solution.py:56
  92.1 6.4 all_gather.46
  99.7 8.7 all_gather.48
  109.8 8.7 all_gather.50
  121.0 18.4 %all-gather.2 = bf16[8,1,256]{2,1,0:T(2,128)(2,1)S(1)} all-gather(bf16[1,1,256]{2,1,0:T(2,128)(2,1)S(1)} %reshape.439), channel_id=1, replica_groups=mesh['dp'=4,'seq'=8] {'seq'}, dimensions={0}, use_global_device_ids=true | all-gather | bytes 4608 | tf_op jit(solution)/shard_map/all_gather | solution.py:98
  155.7 12.7 %fusion.13 = (f32[12,256]{1,0:T(8,128)S(1)}, f32[12,256,2048]{2,1,0:T(8,128)}) fusion(pred[256,2048]{1,0:T(8,128)(4,1)} %or_and_fusion.1, bf16[256,12,64]{0,2,1:T(8,128)(2,1)S(1)} %bitcast.171, bf16[2048,12,64]{0,2,1:T(8,128)(2,1)} %bitcast.173), kind=kOutput, calls=%fused_computation.31 | convolution fusion | flops 824177664 | bytes 29241344 | tf_op jit(solution)/shard_map/qhd,khd->hqk/dot_general | solution.py:103
  168.3 44.0 %all-gather.20.cloned.1.call-done = bf16[2048,1,768]{2,0,1:T(8,128)(2,1)} async-done(((bf16[256,1,768]{2,0,1:T(8,128)(2,1)}), bf16[2048,1,768]{2,0,1:T(8,128)(2,1)}) %all-gather.20.cloned.1.call-update) | async-done | bytes 3145744 | tf_op jit(solution)/shard_map/all_gather | solution.py:97
  217.1 12.9 %fusion.14 = f32[12,256]{1,0:T(8,128)S(1)} fusion(f32[12,256,2048]{2,1,0:T(8,128)} %get-tuple-element.533, f32[12,256]{1,0:T(8,128)S(1)} %broadcast_maximum_fusion, pred[256,2048]{1,0:T(8,128)(4,1)} %or_and_fusion.1), kind=kLoop, calls=%fused_computation.32 | loop fusion | flops 31454208 | bytes 25714688 | tf_op jit(solution)/shard_map/reduce_sum | solution.py:111
  230.6 12.5 %fusion.92 = (bf16[256,12,64]{0,2,1:T(8,128)(2,1)}, f32[256,12,64]{0,2,1:T(8,128)}) fusion(f32[256,12]{0,1:T(8,128)S(1)} %bitcast.190, bf16[2048,12,64]{0,2,1:T(8,128)(2,1)S(1)} %bitcast.179, f32[12,256,2048]{2,1,0:T(8,128)} %get-tuple-element.533, f32[12,256]{1,0:T(8,128)S(1)} %broadcast_maximum_fusion, pred[256,2048]{1,0:T(8,128)(4,1)S(1)} %copy-done.5), kind=kOutput, calls=%fused_computation.188 | convolution fusion | flops 837156864 | bytes 30040064 | tf_op jit(solution)/shard_map/hqk,khd->hqd/dot_general | solution.py:112
  243.2 10.9 all-gather.12.cloned.1.call-done
  257.9 77.5 %all-gather.14.cloned.1.call-done = bf16[768,4,768]{0,2,1:T(8,128)(2,1)} async-done(((bf16[768,4,96]{0,2,1:T(8,128)(2,1)}), bf16[768,4,768]{0,2,1:T(8,128)(2,1)}) %all-gather.14.cloned.1.call-update) | async-done | bytes 4718608 | tf_op jit(solution)/shard_map/all_gather | solution.py:56
  341.8 8.2 multiply_convert_fusion.2
  350.1 66.0 %all-gather.16.cloned.1.call-done = bf16[768,4,768]{0,2,1:T(8,128)(2,1)} async-done(((bf16[768,4,96]{0,2,1:T(8,128)(2,1)}), bf16[768,4,768]{0,2,1:T(8,128)(2,1)}) %all-gather.16.cloned.1.call-update) | async-done | bytes 4718608 | tf_op jit(solution)/shard_map/all_gather | solution.py:64
  438.3 8.7 copy.119
  449.1 253.7 %while.26 = (s32[]{:T(128)}, bf16[256,768]{0,1:T(8,128)(2,1)S(1)}, bf16[256,768]{0,1:T(8,128)(2,1)}, bf16[256]{0:T(256)(128)(2,1)}, f32[256,768]{0,1:T(8,128)S(1...) while((s32[]{:T(128)}, bf16[256,768]{0,1:T(8,128)(2,1)S(1)}, ...), condition=%wide.region_10.11_spmd.clone, body=%wide.region_9.10_spmd.clone.sunk | while | flops 513750016 | bytes 36123720 | solution.py:271
  465.6 15.3 %collective-permute-done.3 = bf16[256,768]{0,1:T(8,128)(2,1)} collective-permute-done((bf16[256,768]{0,1:T(8,128)(2,1)}, bf16[256,768]{0,1:T(8,128)(2,1)}, u32[]{:S(2)}, u32[]{:S(2)}) %collective-permute-start.3) | collective-permute-done | bytes 393248 | tf_op jit(solution)/shard_map/while/body/eval_jaxpr/ppermute | solution.py:29
  502.9 16.9 %collective-permute-done.3 = bf16[256,768]{0,1:T(8,128)(2,1)} collective-permute-done((bf16[256,768]{0,1:T(8,128)(2,1)}, bf16[256,768]{0,1:T(8,128)(2,1)}, u32[]{:S(2)}, u32[]{:S(2)}) %collective-permute-start.3) | collective-permute-done | bytes 393248 | tf_op jit(solution)/shard_map/while/body/eval_jaxpr/ppermute | solution.py:29
  540.0 17.9 %collective-permute-done.3 = bf16[256,768]{0,1:T(8,128)(2,1)} collective-permute-done((bf16[256,768]{0,1:T(8,128)(2,1)}, bf16[256,768]{0,1:T(8,128)(2,1)}, u32[]{:S(2)}, u32[]{:S(2)}) %collective-permute-start.3) | collective-permute-done | bytes 393248 | tf_op jit(solution)/shard_map/while/body/eval_jaxpr/ppermute | solution.py:29
  576.5 17.7 %collective-permute-done.3 = bf16[256,768]{0,1:T(8,128)(2,1)} collective-permute-done((bf16[256,768]{0,1:T(8,128)(2,1)}, bf16[256,768]{0,1:T(8,128)(2,1)}, u32[]{:S(2)}, u32[]{:S(2)}) %collective-permute-start.3) | collective-permute-done | bytes 393248 | tf_op jit(solution)/shard_map/while/body/eval_jaxpr/ppermute | solution.py:29
  612.2 17.2 %collective-permute-done.3 = bf16[256,768]{0,1:T(8,128)(2,1)} collective-permute-done((bf16[256,768]{0,1:T(8,128)(2,1)}, bf16[256,768]{0,1:T(8,128)(2,1)}, u32[]{:S(2)}, u32[]{:S(2)}) %collective-permute-start.3) | collective-permute-done | bytes 393248 | tf_op jit(solution)/shard_map/while/body/eval_jaxpr/ppermute | solution.py:29
  647.1 16.7 %collective-permute-done.3 = bf16[256,768]{0,1:T(8,128)(2,1)} collective-permute-done((bf16[256,768]{0,1:T(8,128)(2,1)}, bf16[256,768]{0,1:T(8,128)(2,1)}, u32[]{:S(2)}, u32[]{:S(2)}) %collective-permute-start.3) | collective-permute-done | bytes 393248 | tf_op jit(solution)/shard_map/while/body/eval_jaxpr/ppermute | solution.py:29
  681.7 15.8 %collective-permute-done.3 = bf16[256,768]{0,1:T(8,128)(2,1)} collective-permute-done((bf16[256,768]{0,1:T(8,128)(2,1)}, bf16[256,768]{0,1:T(8,128)(2,1)}, u32[]{:S(2)}, u32[]{:S(2)}) %collective-permute-start.3) | collective-permute-done | bytes 393248 | tf_op jit(solution)/shard_map/while/body/eval_jaxpr/ppermute | solution.py:29
  745.1 52.8 %all-reduce.3.cloned.1.call-done = bf16[768,4,768]{2,1,0:T(4,128)(2,1)} async-done(((bf16[768,4,768]{2,1,0:T(4,128)(2,1)}), bf16[768,4,768]{2,1,0:T(4,128)(2,1)}) %all-reduce.3.cloned.1.call-update) | async-done | bytes 4718608
  806.3 35.0 %reduce-scatter.16.cloned.1.call-done = bf16[192,3,768]{2,0,1:T(8,128)(2,1)} async-done(((bf16[768,3,768]{2,0,1:T(8,128)(2,1)}), bf16[192,3,768]{2,0,1:T(8,128)(2,1)}) %reduce-scatter.16.cloned.1.call-update) | async-done | bytes 884752 | tf_op jit(solution)/shard_map/reduce_scatter | solution.py:70
  846.5 45.1 %reduce-scatter.20.cloned.1.call-done = bf16[192,4,768]{2,0,1:T(8,128)(2,1)} async-done(((bf16[768,4,768]{2,0,1:T(8,128)(2,1)}), bf16[192,4,768]{2,0,1:T(8,128)(2,1)}) %reduce-scatter.20.cloned.1.call-update) | async-done | bytes 1179664 | tf_op jit(solution)/shard_map/reduce_scatter | solution.py:70
  904.9 39.6 %psum.14 = f32[4,768]{1,0:T(4,128)S(1)} all-reduce(f32[4,768]{1,0:T(4,128)S(1)} %pad_maximum_fusion.4), channel_id=1, replica_groups=mesh['dp'=4,'seq'=8] {'dp','seq'}, use_global_device_ids=true, to_apply=%region_26.27 | all-reduce | flops 3072 | bytes 24576 | tf_op jit(solution)/shard_map/psum | solution.py:297
  945.8 11.4 reduce-scatter.24.cloned.1.call-done
  958.2 66.3 %reduce-scatter.28.cloned.1.call-done = bf16[96,768]{1,0:T(8,128)(2,1)} async-done(((bf16[768,768]{1,0:T(8,128)(2,1)}), bf16[96,768]{1,0:T(8,128)(2,1)}) %reduce-scatter.28.cloned.1.call-update) | async-done | bytes 147472
  1025.8 65.3 %reduce-scatter.22.cloned.1.call-done = bf16[96,576]{1,0:T(8,128)(2,1)} async-done(((bf16[768,576]{1,0:T(8,128)(2,1)}), bf16[96,576]{1,0:T(8,128)(2,1)}) %reduce-scatter.22.cloned.1.call-update) | async-done | bytes 110608
  1092.3 65.7 %reduce-scatter.26.cloned.1.call-done = bf16[96,768]{1,0:T(8,128)(2,1)} async-done(((bf16[768,768]{1,0:T(8,128)(2,1)}), bf16[96,768]{1,0:T(8,128)(2,1)}) %reduce-scatter.26.cloned.1.call-update) | async-done | bytes 147472
  1163.3 39.8 %psum.15 = f32[]{:T(128)} all-reduce(f32[]{:T(128)S(6)} %add.292), channel_id=1, replica_groups=mesh['dp'=4,'seq'=8] {'dp','seq'}, use_global_device_ids=true, to_apply=%region_28.29 | all-reduce | flops 1 | bytes 8 | tf_op jit(solution)/shard_map/psum | solution.py:302
  (439 shorter events, 286.6 us)
Async XLA Ops:
  7.2 79.6 %all-gather.10.cloned.1.call-start = ((), (), s32[]{:S(2)}) async-start(), calls=%async_computation.7 | async-start | bytes 3981312 | tf_op jit(solution)/shard_map/all_gather | solution.py:56
  20.6 129.9 %all-gather.18.cloned.1.call-start = ((), (), s32[]{:S(2)}) async-start(), calls=%async_computation.14 | async-start | bytes 3538944 | tf_op jit(solution)/shard_map/all_gather | solution.py:96
  91.2 121.1 %all-gather.20.cloned.1.call-start = ((), (), s32[]{:S(2)}) async-start(), calls=%async_computation.15 | async-start | bytes 3538944 | tf_op jit(solution)/shard_map/all_gather | solution.py:97
  92.0 162.1 %all-gather.12.cloned.1.call-start = ((), (), s32[]{:S(2)}) async-start(), calls=%async_computation.8 | async-start | bytes 1327104 | tf_op jit(solution)/shard_map/all_gather | solution.py:56
  99.5 235.9 %all-gather.14.cloned.1.call-start = ((), (), s32[]{:S(2)}) async-start(), calls=%async_computation.9 | async-start | bytes 5308416 | tf_op jit(solution)/shard_map/all_gather | solution.py:56
  109.7 306.4 %all-gather.16.cloned.1.call-start = ((), (), s32[]{:S(2)}) async-start(), calls=%async_computation.10 | async-start | bytes 5308416 | tf_op jit(solution)/shard_map/all_gather | solution.py:64
  119.7 621.1 %reduce-scatter.18.cloned.1.call-start = ((), (), s32[]{:S(2)}) async-start(), calls=%async_computation.12 | async-start | bytes 1474560 | tf_op jit(solution)/shard_map/reduce_scatter | solution.py:70
  433.2 364.8 %all-reduce.3.cloned.1.call-start = ((), (), s32[]{:S(2)}) async-start(), calls=%async_computation.20 | async-start | bytes 9437184
  449.1 38.9 %collective-permute-start = (bf16[256,768]{0,1:T(8,128)(2,1)S(1)}, bf16[256,768]{0,1:T(8,128)(2,1)S(1)}, u32[]{:S(2)}, u32[]{:S(2)}) collective-permute-start(bf16[256,768]{0,1:T(8,128)(2,1)S(1)} %copy.148), channel_id=1, source_target_pairs={{0,1},{1,2},{2,3},{3,4},{4,5},{5,6},{6,7},{7,0},{8,9},{9,10},{10,1... | collective-permute-start | bytes 1179656 | tf_op jit(solution)/shard_map/while/body/eval_jaxpr/ppermute | solution.py:29
  451.3 36.7 %collective-permute-start.1 = (bf16[256,768]{0,1:T(8,128)(2,1)}, bf16[256,768]{0,1:T(8,128)(2,1)}, u32[]{:S(2)}, u32[]{:S(2)}) collective-permute-start(bf16[256,768]{0,1:T(8,128)(2,1)} %copy.149), channel_id=1, source_target_pairs={{0,1},{1,2},{2,3},{3,4},{4,5},{5,6},{6,7},{7,0},{8,9},{9,10},{10,1... | collective-permute-start | bytes 1179656 | tf_op jit(solution)/shard_map/while/body/eval_jaxpr/ppermute | solution.py:29
  453.3 34.7 %collective-permute-start.2 = (bf16[256]{0:T(256)(128)(2,1)S(1)}, bf16[256]{0:T(256)(128)(2,1)}, u32[]{:S(2)}, u32[]{:S(2)}) collective-permute-start(bf16[256]{0:T(256)(128)(2,1)S(1)} %copy.150), channel_id=1, source_target_pairs={{0,1},{1,2},{2,3},{3,4},{4,5},{5,6},{6,7},{7,0},{8,9},{9,10},{10,1... | collective-permute-start | bytes 1544 | tf_op jit(solution)/shard_map/while/body/eval_jaxpr/ppermute | solution.py:29
  488.1 38.0 %collective-permute-start = (bf16[256,768]{0,1:T(8,128)(2,1)S(1)}, bf16[256,768]{0,1:T(8,128)(2,1)S(1)}, u32[]{:S(2)}, u32[]{:S(2)}) collective-permute-start(bf16[256,768]{0,1:T(8,128)(2,1)S(1)} %copy.148), channel_id=1, source_target_pairs={{0,1},{1,2},{2,3},{3,4},{4,5},{5,6},{6,7},{7,0},{8,9},{9,10},{10,1... | collective-permute-start | bytes 1179656 | tf_op jit(solution)/shard_map/while/body/eval_jaxpr/ppermute | solution.py:29
  489.9 36.2 %collective-permute-start.1 = (bf16[256,768]{0,1:T(8,128)(2,1)}, bf16[256,768]{0,1:T(8,128)(2,1)}, u32[]{:S(2)}, u32[]{:S(2)}) collective-permute-start(bf16[256,768]{0,1:T(8,128)(2,1)} %copy.149), channel_id=1, source_target_pairs={{0,1},{1,2},{2,3},{3,4},{4,5},{5,6},{6,7},{7,0},{8,9},{9,10},{10,1... | collective-permute-start | bytes 1179656 | tf_op jit(solution)/shard_map/while/body/eval_jaxpr/ppermute | solution.py:29
  490.6 35.5 %collective-permute-start.2 = (bf16[256]{0:T(256)(128)(2,1)S(1)}, bf16[256]{0:T(256)(128)(2,1)}, u32[]{:S(2)}, u32[]{:S(2)}) collective-permute-start(bf16[256]{0:T(256)(128)(2,1)S(1)} %copy.150), channel_id=1, source_target_pairs={{0,1},{1,2},{2,3},{3,4},{4,5},{5,6},{6,7},{7,0},{8,9},{9,10},{10,1... | collective-permute-start | bytes 1544 | tf_op jit(solution)/shard_map/while/body/eval_jaxpr/ppermute | solution.py:29
  526.1 37.1 %collective-permute-start = (bf16[256,768]{0,1:T(8,128)(2,1)S(1)}, bf16[256,768]{0,1:T(8,128)(2,1)S(1)}, u32[]{:S(2)}, u32[]{:S(2)}) collective-permute-start(bf16[256,768]{0,1:T(8,128)(2,1)S(1)} %copy.148), channel_id=1, source_target_pairs={{0,1},{1,2},{2,3},{3,4},{4,5},{5,6},{6,7},{7,0},{8,9},{9,10},{10,1... | collective-permute-start | bytes 1179656 | tf_op jit(solution)/shard_map/while/body/eval_jaxpr/ppermute | solution.py:29
  528.0 35.2 %collective-permute-start.1 = (bf16[256,768]{0,1:T(8,128)(2,1)}, bf16[256,768]{0,1:T(8,128)(2,1)}, u32[]{:S(2)}, u32[]{:S(2)}) collective-permute-start(bf16[256,768]{0,1:T(8,128)(2,1)} %copy.149), channel_id=1, source_target_pairs={{0,1},{1,2},{2,3},{3,4},{4,5},{5,6},{6,7},{7,0},{8,9},{9,10},{10,1... | collective-permute-start | bytes 1179656 | tf_op jit(solution)/shard_map/while/body/eval_jaxpr/ppermute | solution.py:29
  528.6 34.6 %collective-permute-start.2 = (bf16[256]{0:T(256)(128)(2,1)S(1)}, bf16[256]{0:T(256)(128)(2,1)}, u32[]{:S(2)}, u32[]{:S(2)}) collective-permute-start(bf16[256]{0:T(256)(128)(2,1)S(1)} %copy.150), channel_id=1, source_target_pairs={{0,1},{1,2},{2,3},{3,4},{4,5},{5,6},{6,7},{7,0},{8,9},{9,10},{10,1... | collective-permute-start | bytes 1544 | tf_op jit(solution)/shard_map/while/body/eval_jaxpr/ppermute | solution.py:29
  563.3 36.1 %collective-permute-start = (bf16[256,768]{0,1:T(8,128)(2,1)S(1)}, bf16[256,768]{0,1:T(8,128)(2,1)S(1)}, u32[]{:S(2)}, u32[]{:S(2)}) collective-permute-start(bf16[256,768]{0,1:T(8,128)(2,1)S(1)} %copy.148), channel_id=1, source_target_pairs={{0,1},{1,2},{2,3},{3,4},{4,5},{5,6},{6,7},{7,0},{8,9},{9,10},{10,1... | collective-permute-start | bytes 1179656 | tf_op jit(solution)/shard_map/while/body/eval_jaxpr/ppermute | solution.py:29
  565.1 34.3 %collective-permute-start.1 = (bf16[256,768]{0,1:T(8,128)(2,1)}, bf16[256,768]{0,1:T(8,128)(2,1)}, u32[]{:S(2)}, u32[]{:S(2)}) collective-permute-start(bf16[256,768]{0,1:T(8,128)(2,1)} %copy.149), channel_id=1, source_target_pairs={{0,1},{1,2},{2,3},{3,4},{4,5},{5,6},{6,7},{7,0},{8,9},{9,10},{10,1... | collective-permute-start | bytes 1179656 | tf_op jit(solution)/shard_map/while/body/eval_jaxpr/ppermute | solution.py:29
  565.7 33.7 %collective-permute-start.2 = (bf16[256]{0:T(256)(128)(2,1)S(1)}, bf16[256]{0:T(256)(128)(2,1)}, u32[]{:S(2)}, u32[]{:S(2)}) collective-permute-start(bf16[256]{0:T(256)(128)(2,1)S(1)} %copy.150), channel_id=1, source_target_pairs={{0,1},{1,2},{2,3},{3,4},{4,5},{5,6},{6,7},{7,0},{8,9},{9,10},{10,1... | collective-permute-start | bytes 1544 | tf_op jit(solution)/shard_map/while/body/eval_jaxpr/ppermute | solution.py:29
  599.5 35.2 %collective-permute-start = (bf16[256,768]{0,1:T(8,128)(2,1)S(1)}, bf16[256,768]{0,1:T(8,128)(2,1)S(1)}, u32[]{:S(2)}, u32[]{:S(2)}) collective-permute-start(bf16[256,768]{0,1:T(8,128)(2,1)S(1)} %copy.148), channel_id=1, source_target_pairs={{0,1},{1,2},{2,3},{3,4},{4,5},{5,6},{6,7},{7,0},{8,9},{9,10},{10,1... | collective-permute-start | bytes 1179656 | tf_op jit(solution)/shard_map/while/body/eval_jaxpr/ppermute | solution.py:29
  601.3 33.4 %collective-permute-start.1 = (bf16[256,768]{0,1:T(8,128)(2,1)}, bf16[256,768]{0,1:T(8,128)(2,1)}, u32[]{:S(2)}, u32[]{:S(2)}) collective-permute-start(bf16[256,768]{0,1:T(8,128)(2,1)} %copy.149), channel_id=1, source_target_pairs={{0,1},{1,2},{2,3},{3,4},{4,5},{5,6},{6,7},{7,0},{8,9},{9,10},{10,1... | collective-permute-start | bytes 1179656 | tf_op jit(solution)/shard_map/while/body/eval_jaxpr/ppermute | solution.py:29
  601.9 32.8 %collective-permute-start.2 = (bf16[256]{0:T(256)(128)(2,1)S(1)}, bf16[256]{0:T(256)(128)(2,1)}, u32[]{:S(2)}, u32[]{:S(2)}) collective-permute-start(bf16[256]{0:T(256)(128)(2,1)S(1)} %copy.150), channel_id=1, source_target_pairs={{0,1},{1,2},{2,3},{3,4},{4,5},{5,6},{6,7},{7,0},{8,9},{9,10},{10,1... | collective-permute-start | bytes 1544 | tf_op jit(solution)/shard_map/while/body/eval_jaxpr/ppermute | solution.py:29
  634.8 34.5 %collective-permute-start = (bf16[256,768]{0,1:T(8,128)(2,1)S(1)}, bf16[256,768]{0,1:T(8,128)(2,1)S(1)}, u32[]{:S(2)}, u32[]{:S(2)}) collective-permute-start(bf16[256,768]{0,1:T(8,128)(2,1)S(1)} %copy.148), channel_id=1, source_target_pairs={{0,1},{1,2},{2,3},{3,4},{4,5},{5,6},{6,7},{7,0},{8,9},{9,10},{10,1... | collective-permute-start | bytes 1179656 | tf_op jit(solution)/shard_map/while/body/eval_jaxpr/ppermute | solution.py:29
  636.6 32.7 %collective-permute-start.1 = (bf16[256,768]{0,1:T(8,128)(2,1)}, bf16[256,768]{0,1:T(8,128)(2,1)}, u32[]{:S(2)}, u32[]{:S(2)}) collective-permute-start(bf16[256,768]{0,1:T(8,128)(2,1)} %copy.149), channel_id=1, source_target_pairs={{0,1},{1,2},{2,3},{3,4},{4,5},{5,6},{6,7},{7,0},{8,9},{9,10},{10,1... | collective-permute-start | bytes 1179656 | tf_op jit(solution)/shard_map/while/body/eval_jaxpr/ppermute | solution.py:29
  669.3 33.4 %collective-permute-start = (bf16[256,768]{0,1:T(8,128)(2,1)S(1)}, bf16[256,768]{0,1:T(8,128)(2,1)S(1)}, u32[]{:S(2)}, u32[]{:S(2)}) collective-permute-start(bf16[256,768]{0,1:T(8,128)(2,1)S(1)} %copy.148), channel_id=1, source_target_pairs={{0,1},{1,2},{2,3},{3,4},{4,5},{5,6},{6,7},{7,0},{8,9},{9,10},{10,1... | collective-permute-start | bytes 1179656 | tf_op jit(solution)/shard_map/while/body/eval_jaxpr/ppermute | solution.py:29
  705.7 135.6 %reduce-scatter.16.cloned.1.call-start = ((), (), s32[]{:S(2)}) async-start(), calls=%async_computation.11 | async-start | bytes 4423680 | tf_op jit(solution)/shard_map/reduce_scatter | solution.py:70
  735.3 156.3 %reduce-scatter.20.cloned.1.call-start = ((), (), s32[]{:S(2)}) async-start(), calls=%async_computation.13 | async-start | bytes 5898240 | tf_op jit(solution)/shard_map/reduce_scatter | solution.py:70
  740.7 216.5 %reduce-scatter.24.cloned.1.call-start = ((), (), s32[]{:S(2)}) async-start(), calls=%async_computation.17 | async-start | bytes 442368
  743.8 280.7 %reduce-scatter.28.cloned.1.call-start = ((), (), s32[]{:S(2)}) async-start(), calls=%async_computation.19 | async-start | bytes 1327104
  806.3 284.8 %reduce-scatter.22.cloned.1.call-start = ((), (), s32[]{:S(2)}) async-start(), calls=%async_computation.16 | async-start | bytes 1105920
  846.2 311.9 %reduce-scatter.26.cloned.1.call-start = ((), (), s32[]{:S(2)}) async-start(), calls=%async_computation.18 | async-start | bytes 1327104
  (81 other events, 2730.6 us)
Sparse Core Ops, SparseCore 0:
  20.7 66.0 all-gather.9
  91.4 59.0 all-gather.17
  153.2 59.0 all-gather.19
  214.4 39.6 all-gather.11
  256.7 78.6 all-gather.13
  338.0 78.0 all-gather.15
  433.3 23.8 reduce-scatter.17
  705.8 92.0 all-reduce.2
  800.7 40.5 reduce-scatter.15
  843.7 47.8 reduce-scatter.19
  895.7 61.4 reduce-scatter.23
  961.4 63.0 reduce-scatter.27
  1028.8 62.2 reduce-scatter.21
  1094.9 63.1 reduce-scatter.25
where the time goes:
time: 1220 us
  waiting for transfers between devices  762 us (62%)
  blocking collectives  132 us (11%)
  matrix products  124 us (10%)
  local copies, waits for them, and re-layouts  84.9 us (7%)
  other arithmetic  73.7 us (6%)
  starting transfers between devices  19.7 us (2%)
  between operations  19.6 us (2%)
    unnamed x19, waiting for transfers between devices  263 us
    all_gather x3, waiting for transfers between devices, spread_blocks(): lax.all_gather(gathered, 'seq', axis=2, tiled=True)  154 us
    ppermute x37, waiting for transfers between devices, shifted_2(): return lax.ppermute(x, axis, [(i, (i + by) % count) for i in range(count)])  151 us
    reduce_scatter x3, waiting for transfers between devices, reduce_grads(): lax.psum_scatter(jnp.einsum('td,tbc->dbc', left, right, preferred_element...  80.1 us
    all_gather x1, waiting for transfers between devices, collect_blocks(): pieces = lax.all_gather(gathered, 'seq', axis=2, tiled=True)  66 us
    all_gather x1, waiting for transfers between devices, attend_forward(): values_here = lax.all_gather(value_rows, 'seq', axis=0, tiled=True)  44 us
    psum x1, blocking collectives, local(): grad_norm = jnp.sqrt(lax.psum(squares, ('dp', 'seq')))  39.8 us
    psum x1, blocking collectives, local(): lax.psum(jnp.stack([gain_one_grad, shift_one_grad, gain_two_grad, shift_t...  39.6 us
  transfers between devices with their start and end apart: 51, of which 29 were waited for; matrix products, arithmetic and copies ran while one was open for 20% of the time, Pallas kernels for 0%

commit v1 on v0

v1 whole, which is shorter than its diff:
```python
import math
from functools import partial

import jax
import jax.numpy as jnp
from jax import lax
from jax.sharding import PartitionSpec as P

D = 768
HEADS = 12
HEAD_DIM = 64
FF = 3072
VIEW = 1024
STEP = 10
GROUPS = 4
GROUP_HEADS = HEADS // GROUPS
GROUP_WIDTH = GROUP_HEADS * HEAD_DIM
WIDE = FF // D
RING = (0, 1, 3, 2)

layer_eps = 1e-05
beta_first = 0.9
beta_second = 0.95
adam_eps = 1e-08
rate_matrix = 0.08
rate_vector = 0.8
weight_decay = 0.1
masked_score = -1e30
bf16 = jnp.bfloat16
f32 = jnp.float32


def gray(v):
    return v ^ (v >> 1)


def hop_quarter(value, by):
    split = lax.axis_size("seq") // GROUPS
    pairs = [
        (RING[p] * split + x, RING[(p + by) % GROUPS] * split + x) for p in range(GROUPS) for x in range(split)
    ]
    return lax.ppermute(value, "seq", pairs)


def hop_within(value, by):
    split = lax.axis_size("seq") // GROUPS
    pairs = [(q * split + x, q * split + (x + by) % split) for q in range(GROUPS) for x in range(split)]
    return lax.ppermute(value, "seq", pairs)


def swap(value, axis, bit):
    return lax.ppermute(value, axis, [(i, i ^ bit) for i in range(lax.axis_size(axis))])


def bits_of(axis):
    return [1 << b for b in range(lax.axis_size(axis).bit_length() - 1)]


def total(value):
    for axis in ("dp", "seq"):
        for bit in bits_of(axis):
            value = value + swap(value, axis, bit)
    return value


def pick(stack, index):
    return lax.dynamic_index_in_dim(stack, index, 0, keepdims=False)


def layer_stats(values):
    centre = jnp.mean(values, axis=-1, keepdims=True)
    shifted = values - centre
    spread = jnp.mean(shifted * shifted, axis=-1, keepdims=True)
    inverse = lax.rsqrt(spread + layer_eps)
    return (shifted * inverse, inverse)


def layer_back(grad_normed, normalized, inverse, gain):
    scaled = grad_normed * gain
    centred = jnp.mean(scaled, axis=-1, keepdims=True)
    along = jnp.mean(scaled * normalized, axis=-1, keepdims=True)
    return inverse * (scaled - centred - normalized * along)


def mm(a, b):
    return jnp.dot(a, b, preferred_element_type=f32)


def mm_nt(a, b):
    return lax.dot_general(a, b, (((1,), (1,)), ((), ())), preferred_element_type=f32)


def mm_tn(a, b):
    return lax.dot_general(a, b, (((0,), (0,)), ((), ())), preferred_element_type=f32)


def gather_rows(piece):
    for bit in reversed(bits_of("dp")):
        piece = jnp.concatenate([piece, swap(piece, "dp", bit)], axis=1)
    return piece


def row_order():
    order = [0]
    for bit in reversed(bits_of("dp")):
        order = order + [o ^ bit for o in order]
    return order


def reduce_rows(piece):
    for bit in bits_of("dp"):
        half = piece.shape[1] // 2
        there = swap(piece[:, half:], "dp", bit)
        piece = (piece[:, :half].astype(f32) + there.astype(f32)).astype(bf16)
    return piece


def reduce_within(piece):
    own = piece[0].astype(f32)
    for j in range(1, piece.shape[0]):
        own = own + hop_within(piece[j], -j).astype(f32)
    return own.astype(bf16)


def reduce_ring(slots):
    moving = slots[1]
    for k in (2, 3):
        moving = (hop_quarter(moving, 1).astype(f32) + slots[k].astype(f32)).astype(bf16)
    return hop_quarter(moving, 1).astype(f32) + slots[0].astype(f32)


def adam_step(params, grads, first, second, rate, decay):
    first_new = beta_first * first + (1.0 - beta_first) * grads
    second_new = beta_second * second + (1.0 - beta_second) * grads * grads
    first_hat = first_new / (1.0 - beta_first**STEP)
    second_hat = second_new / (1.0 - beta_second**STEP)
    params_new = params - rate * (first_hat / (jnp.sqrt(second_hat) + adam_eps) + decay * params)
    return (params_new, first_new, second_new)


def local(
    patches,
    cotangent,
    input_views,
    token_live,
    master,
    moment_one,
    moment_two,
    norm_params,
    norm_moment_one,
    norm_moment_two,
):
    tokens = patches.shape[0]
    rows, blocks, cols = master.shape
    n_dp = lax.axis_size("dp")
    split = lax.axis_size("seq") // GROUPS
    dp = lax.axis_index("dp")
    seq = lax.axis_index("seq")
    quarter, within = seq // split, seq % split
    place = gray(quarter)
    inputs_seen = input_views[0]
    gain_one, shift_one, gain_two, shift_two = (norm_params[i] for i in range(4))
    order = row_order()
    dp_place = [order.index(a) for a in range(n_dp)]

    def quarter_behind(k):
        return gray((place - k) & 3)

    flags = jnp.pad(token_live.astype(bf16)[None, :], ((0, 7), (0, D - tokens)))
    ring = [jnp.concatenate([patches, flags], axis=0)]
    for _ in range(3):
        ring.append(hop_quarter(ring[-1], 1))
    pieces = [[ring[k]] + [hop_within(ring[k], j) for j in range(1, split)] for k in range(4)]
    scene = jnp.stack([jnp.stack([p[:tokens] for p in pieces[k]]) for k in range(4)])
    live = jnp.stack([jnp.concatenate([p[tokens, :tokens] for p in pieces[k]]) for k in range(4)])

    copy_low = master.astype(bf16)
    mine = copy_low[:, 0:3, :].reshape(rows, 3 * cols)
    near = jnp.stack([mine] + [hop_within(mine, j) for j in range(1, split)])
    near = gather_rows(near).reshape(split, n_dp, rows, 3, cols)
    near = jnp.stack([pick(near, (within - a) % split) for a in range(split)])
    near = jnp.moveaxis(near, 1, 0)
    near = jnp.stack([pick(near, order_at) for order_at in [relative(dp, a, order) for a in range(n_dp)]])
    w_qkv = jnp.transpose(near, (0, 2, 3, 1, 4)).reshape(D, 3, GROUP_WIDTH)

    up = copy_low[:, 4 : 4 + WIDE].reshape(rows, WIDE * cols)
    down = copy_low[:, 4 + WIDE :].reshape(rows, WIDE * cols)
    far = [jnp.concatenate([up, down, copy_low[:, 3]], axis=1)]
    for _ in range(3):
        far.append(hop_quarter(far[-1], 1))
    weights = [gather_rows(jnp.stack([f] + [hop_within(f, j) for j in range(1, split)])) for f in far]
    width = WIDE * cols
    w_up = [w[:, :, :width] for w in weights]
    w_down = [w[:, :, width : 2 * width] for w in weights]
    w_out = jnp.stack([w[:, :, 2 * width :] for w in weights]).reshape(4 * split, n_dp, rows, cols)

    def slot_of(quarter_abs, within_abs):
        return ((place - gray(quarter_abs)) & 3) * split + (within - within_abs) % split

    w_out = jnp.stack([pick(w_out, slot_of(a // split, a % split)) for a in range(4 * split)])
    w_out = jnp.moveaxis(w_out, 1, 0)
    w_out = jnp.stack([pick(w_out, relative(dp, a, order)) for a in range(n_dp)])
    w_out = jnp.transpose(w_out, (0, 2, 1, 3)).reshape(D, D)

    normal_one, inverse_one = layer_stats(scene.astype(f32))
    act_one = (normal_one * gain_one + shift_one).astype(bf16)
    act_all = act_one.reshape(4 * split * tokens, D)
    act_own = act_one[:, 0].reshape(4 * tokens, D)
    q = mm(act_own, w_qkv[:, 0]).astype(bf16)
    k = mm(act_all, w_qkv[:, 1]).astype(bf16)
    v = mm(act_all, w_qkv[:, 2]).astype(bf16)

    def heads(m):
        return jnp.transpose(m.reshape(m.shape[0], GROUP_HEADS, HEAD_DIM), (1, 0, 2))

    def unheads(m):
        return jnp.transpose(m, (1, 0, 2)).reshape(m.shape[1], GROUP_WIDTH)

    views = jnp.stack([(quarter_behind(i) * split * tokens) // VIEW for i in range(4)])
    open_block = (views[None, :] < inputs_seen) | (views[None, :] == views[:, None])
    visible = open_block[:, None, :, None] & (live > 0)[None, None]
    visible = jnp.broadcast_to(visible, (4, tokens, 4, split * tokens)).reshape(4 * tokens, -1)
    scaling = 1.0 / math.sqrt(HEAD_DIM)
    qh, kh, vh = heads(q), heads(k), heads(v)
    scores = jnp.einsum("hqd,hkd->hqk", qh, kh, preferred_element_type=f32) * scaling
    scores = jnp.where(visible[None], scores, masked_score)
    top = jnp.max(scores, axis=-1, keepdims=True)
    probs = jnp.where(visible[None], jnp.exp(scores - top), 0.0)
    probs = probs / jnp.sum(probs, axis=-1, keepdims=True)
    probs_low = probs.astype(bf16)
    attended = jnp.einsum("hqk,hkd->hqd", probs_low, vh, preferred_element_type=f32)
    flat = unheads(attended).astype(bf16).reshape(4, tokens, GROUP_WIDTH)
    back = jnp.stack([flat[0]] + [hop_quarter(flat[i], -i) for i in range(1, 4)])
    act_two = jnp.concatenate([pick(back, (gray(a) - place) & 3) for a in range(4)], axis=1)

    patch_float = patches.astype(f32)
    resid = patch_float + mm(act_two, w_out)
    normal_two, inverse_two = layer_stats(resid)
    act_three = (normal_two * gain_two + shift_two).astype(bf16)

    def to_relative(m):
        parts = m.reshape(tokens, n_dp, rows)
        return jnp.concatenate([lax.dynamic_index_in_dim(parts, dp ^ o, 1, keepdims=False) for o in order], axis=1)

    def from_relative(m):
        parts = m.reshape(tokens, n_dp, rows)
        return jnp.concatenate(
            [lax.dynamic_index_in_dim(parts, relative(dp, a, order), 1, keepdims=False) for a in range(n_dp)], axis=1
        )

    act_rel = to_relative(act_three)
    cot_rel = to_relative(cotangent)
    branch_rel = jnp.zeros((tokens, D), f32)
    three_rel = jnp.zeros((tokens, D), f32)
    far_grads = []
    for i in range(4):
        group = []
        for j in range(split):
            widened = mm(act_rel, w_up[i][j])
            activated, gelu_pull = jax.vjp(partial(jax.nn.gelu, approximate=False), widened)
            hidden = activated.astype(bf16)
            branch_rel = branch_rel + mm_nt(hidden, w_down[i][j])
            grad_wide = gelu_pull(mm(cot_rel, w_down[i][j]))[0].astype(bf16)
            three_rel = three_rel + mm_nt(grad_wide, w_up[i][j])
            grad_up = mm_tn(act_rel, grad_wide).astype(bf16)
            grad_down = mm_tn(cot_rel, hidden).astype(bf16)
            group.append((grad_up, grad_down))
        far_grads.append(group)
    block_out = (resid + from_relative(branch_rel)).astype(bf16)
    grad_three = from_relative(three_rel)
    gain_two_grad = jnp.sum(grad_three * normal_two, axis=0)
    shift_two_grad = jnp.sum(grad_three, axis=0)
    grad_resid = cotangent.astype(f32) + layer_back(grad_three, normal_two, inverse_two, gain_two)
    grad_branch = grad_resid.astype(bf16)
    grad_attended = mm_nt(grad_branch, w_out).astype(bf16)
    grad_w_out = mm_tn(act_two, grad_branch).astype(bf16)

    parts = jnp.transpose(grad_attended.reshape(tokens, 4, GROUP_WIDTH), (1, 0, 2))
    parts = [pick(parts, gray((place + i) & 3)) for i in range(4)]
    grad_here = jnp.concatenate([parts[0]] + [hop_quarter(parts[i], i) for i in range(1, 4)], axis=0)
    gh = heads(grad_here)
    dprobs = jnp.einsum("hqd,hkd->hqk", gh, vh, preferred_element_type=f32)
    delta = jnp.sum(gh.astype(f32) * attended, axis=-1, keepdims=True)
    grad_scores = (probs * (dprobs - delta)).astype(bf16)
    dq = unheads(jnp.einsum("hqk,hkd->hqd", grad_scores, kh, preferred_element_type=f32) * scaling).astype(bf16)
    dk = unheads(jnp.einsum("hqk,hqd->hkd", grad_scores, qh, preferred_element_type=f32) * scaling).astype(bf16)
    dv = unheads(jnp.einsum("hqk,hqd->hkd", probs_low, gh, preferred_element_type=f32)).astype(bf16)

    grad_near = jnp.stack([mm_tn(act_own, dq), mm_tn(act_all, dk), mm_tn(act_all, dv)], axis=1).astype(bf16)
    grad_near = grad_near.reshape(n_dp, rows, 3, split, cols)
    grad_near = jnp.stack([pick(grad_near, dp ^ o) for o in order])
    grad_near = jnp.transpose(grad_near, (3, 0, 1, 2, 4)).reshape(split, D, 3 * cols)
    grad_near = jnp.stack([pick(grad_near, (within - j) % split) for j in range(split)])
    grad_near = reduce_within(reduce_rows(grad_near)).astype(f32).reshape(rows, 3, cols)

    one_q = mm_nt(dq, w_qkv[:, 0]).reshape(4, 1, tokens, D)
    one_kv = (mm_nt(dk, w_qkv[:, 1]) + mm_nt(dv, w_qkv[:, 2])).reshape(4, split, tokens, D)
    one = jnp.concatenate([one_kv[:, :1] + one_q, one_kv[:, 1:]], axis=1)
    gain_one_grad = jnp.sum(one * normal_one, axis=(0, 1, 2))
    shift_one_grad = jnp.sum(one, axis=(0, 1, 2))
    one_low = one.astype(bf16)
    grad_one = reduce_ring([reduce_within(one_low[i]) for i in range(4)])
    patches_grad = grad_resid + layer_back(grad_one, normal_one[0, 0], inverse_one[0, 0], gain_one)

    out_parts = grad_w_out.reshape(n_dp, rows, 4 * split, cols)
    out_parts = jnp.stack([pick(out_parts, dp ^ o) for o in order])
    out_parts = jnp.transpose(out_parts, (2, 0, 1, 3)).reshape(4 * split, D, cols)
    slots = []
    for i in range(4):
        stack = []
        for j in range(split):
            own_out = pick(out_parts, quarter_behind(i) * split + (within - j) % split)
            stack.append(jnp.concatenate([*far_grads[i][j], own_out], axis=1))
        slots.append(reduce_within(reduce_rows(jnp.stack(stack))))
    far_sum = reduce_ring(slots)
    grad_up = far_sum[:, :width].reshape(rows, WIDE, cols)
    grad_down = far_sum[:, width : 2 * width].reshape(rows, WIDE, cols)
    grad_out = far_sum[:, 2 * width :].reshape(rows, 1, cols)

    weight_grad = jnp.concatenate([grad_near, grad_out, grad_up, grad_down], axis=1)
    param_grad = total(jnp.stack([gain_one_grad, shift_one_grad, gain_two_grad, shift_two_grad]))
    squares = total(jnp.full((8, 128), jnp.sum(weight_grad * weight_grad), f32))[0, 0] + jnp.sum(param_grad * param_grad)
    grad_norm = jnp.sqrt(squares)
    clip = 1.0 / jnp.maximum(grad_norm, 1.0)
    new_master, new_moment_one, new_moment_two = adam_step(
        master, weight_grad * clip, moment_one, moment_two, rate_matrix, weight_decay
    )
    new_norm_params, new_norm_moment_one, new_norm_moment_two = adam_step(
        norm_params, param_grad * clip, norm_moment_one, norm_moment_two, rate_vector, 0.0
    )
    return (
        block_out,
        patches_grad,
        new_master,
        new_master.astype(bf16),
        new_moment_one,
        new_moment_two,
        new_norm_params,
        new_norm_moment_one,
        new_norm_moment_two,
        grad_norm,
    )


def relative(dp, absolute, order):
    index = jnp.int32(0)
    for at, offset in enumerate(order):
        index = jnp.where((dp ^ absolute) == offset, at, index)
    return index


def solution(mesh):
    tokens = P(("dp", "seq"), None)
    weights = P("dp", None, "seq")
    return jax.shard_map(
        local,
        mesh=mesh,
        in_specs=(tokens, tokens, P("dp"), P(("dp", "seq")), weights, weights, weights, P(), P(), P()),
        out_specs=(tokens, tokens, weights, weights, weights, weights, P(), P(), P(), P()),
        check_vma=False,
    )
```

time: 1220 us -> 656 us (0.54)
  waiting for transfers between devices: 762 us -> 89.4 us
  blocking collectives: 132 us -> 0 us
  local copies, waits for them, and re-layouts: 84.9 us -> 216 us
  other arithmetic: 73.7 us -> 138 us
  starting transfers between devices: 19.7 us -> 60 us
  between operations: 19.6 us -> 6.53 us
    all_gather x6 -> x0, waiting for transfers between devices: 268 us -> none  [the longest x3 154 us: spread_blocks(): lax.all_gather(gathered, 'seq', axis=2, tiled=True)]
    unnamed x19 -> x0, waiting for transfers between devices: 263 us -> none
    reduce_scatter x3 -> x0, waiting for transfers between devices: 80.1 us -> none  [reduce_grads(): lax.psum_scatter(jnp.einsum('td,tbc->dbc', left, right, preferred_element...]
    psum x2 -> x0, blocking collectives: 79.4 us -> none  [the longest x1 39.8 us: local(): grad_norm = jnp.sqrt(lax.psum(squares, ('dp', 'seq')))]
    ppermute x37 -> x66, waiting for transfers between devices: 151 us -> 89.4 us  [the longest x30 41.4 us: swap(): lax.ppermute(value, axis, [(i, i ^ bit) for i in range(lax.axis_size(axis...]
    all_gather x5 -> x0, blocking collectives: 52.4 us -> none  [the longest x4 34 us: full_rows(): return lax.all_gather(blocks, 'dp', axis=0, tiled=True)]
    ppermute x37 -> x66, starting transfers between devices: 18.6 us -> 60 us  [the longest x18 21.7 us: hop_quarter(): return lax.ppermute(value, 'seq', pairs)]
    another operation x0 -> x27, local copies, waits for them, and re-layouts: none -> 38.7 us
  transfers between devices with their start and end apart: 51 -> 66, of which waited for: 29 -> 21; matrix products, arithmetic and copies ran while one was open for 20% -> 53% of each run, Pallas kernels for 0% -> 0%
where the time goes in v1:
time: 656 us; the launch traced here: 644 us
  local copies, waits for them, and re-layouts  216 us (33%)
  other arithmetic  138 us (21%)
  matrix products  134 us (20%)
  waiting for transfers between devices  89.4 us (14%)
  starting transfers between devices  60 us (9%)
    unnamed x376, local copies, waits for them, and re-layouts  45.4 us
    ppermute x30, waiting for transfers between devices, swap(): lax.ppermute(value, axis, [(i, i ^ bit) for i in range(lax.axis_size(axis...  41.4 us
    dot_general x20, matrix products, mm(): return jnp.dot(a, b, preferred_element_type=f32)  25.8 us
    ppermute x18, waiting for transfers between devices, hop_within(): return lax.ppermute(value, 'seq', pairs)  25.8 us
    dot_general x20, matrix products, mm_tn(): lax.dot_general(a, b, (((0,), (0,)), ((), ())), preferred_element_type=f32)  23.5 us
    ppermute x18, waiting for transfers between devices, hop_quarter(): return lax.ppermute(value, 'seq', pairs)  22.2 us
    ppermute x18, starting transfers between devices, hop_quarter(): return lax.ppermute(value, 'seq', pairs)  21.7 us
    ppermute x18, starting transfers between devices, hop_within(): return lax.ppermute(value, 'seq', pairs)  19.3 us
  transfers between devices with their start and end apart: 66, of which 21 were waited for; matrix products, arithmetic and copies ran while one was open for 53% of the time, Pallas kernels for 0%

profile of v1, /device:TPU:0, one launch (start us, length us, event | category | flops | bytes accessed | tf_op | source)
XLA Modules:
  0.0 644.3 jit_solution(12115771700436298943)
XLA Ops:
  15.3 11.9 %collective-permute-done.7 = bf16[192,288]{0,1:T(8,128)(2,1)S(1)} collective-permute-done((bf16[192,288]{0,1:T(8,128)(2,1)S(1)}, bf16[192,288]{0,1:T(8,128)(2,1)S(1)}, u32[]{:S(2)}, u32[]{:S(2)}) %collective-permute-start.7) | collective-permute-done | bytes 110624 | tf_op jit(solution)/shard_map/ppermute | solution.py:48
  56.1 3.7 fusion.47
  93.0 4.3 collective-permute-done.25
  127.5 19.1 %fusion.154 = (f32[3,1024]{1,0:T(4,128)}, f32[3,1024,2048]{2,1,0:T(8,128)}) fusion(pred[1024,2048]{1,0:T(8,128)(4,1)} %bitcast.502, bf16[3,1024,64]{1,2,0:T(8,128)(2,1)S(1)} %bitcast.484, bf16[3,2048,64]{1,2,0:T(8,128)(2,1)} %bitcast.544), kind=kOutput, calls=%fused_computation.522 | convolution fusion | flops 836765696 | bytes 28454912 | tf_op jit(solution)/shard_map/sub | solution.py:228
  146.7 14.2 %fusion.5 = bf16[3,1024,2048]{2,1,0:T(8,128)(2,1)} fusion(f32[3,1024,2048]{2,1,0:T(8,128)} %get-tuple-element.140, f32[3,1024]{1,0:T(4,128)} %get-tuple-element.139), kind=kLoop, calls=%fused_computation.9 | loop fusion | flops 12582912 | bytes 37761024 | tf_op jit(solution)/shard_map/convert_element_type | solution.py:230
  160.9 8.5 %fusion.157 = f32[3,1024,64]{1,2,0:T(8,128)S(1)} fusion(bf16[3,1024,2048]{2,1,0:T(8,128)(2,1)} %fusion.5, bf16[3,2048,64]{1,2,0:T(8,128)(2,1)S(1)} %bitcast.541), kind=kOutput, calls=%fused_computation.525 | convolution fusion | flops 805306368 | bytes 14155776 | tf_op jit(solution)/shard_map/hqk,hkd->hqd/dot_general | solution.py:231
  172.7 3.6 collective-permute-start.11
  186.9 5.3 fusion.9
  193.5 4.8 copy.114
  209.0 3.4 maximum_bitcast_fusion.25
  223.6 4.4 reshape.639
  232.6 4.7 constant_dynamic-slice_fusion.30
  248.9 4.2 reshape.640
  318.5 3.8 multiply_reduce_fusion.3
  350.7 3.6 collective-permute-start.29
  354.2 4.0 reshape.654
  360.1 4.3 constant_dynamic-slice_fusion.1
  393.4 7.9 %convolution_convert_fusion.2 = bf16[3,2048,64]{1,2,0:T(8,128)(2,1)} fusion(bf16[3,1024,2048]{2,1,0:T(8,128)(2,1)} %fusion.5, bf16[256,3,64]{0,2,1:T(8,128)(2,1)} %bitcast.113, bf16[256,3,64]{0,2,1:T(8,128)(2,1)} %bitcast.111, bf16[256,3,64]{0,2,1:T(8,128)(2,1)} %bitcast.109, bf16[256,3,64]{0,2,1:T(8,128)(2,1)S(1)} %bitcast.539), kind=kOutput, calls=%fused_computation.42 | convolution fusion | flops 807272448 | bytes 13762560 | tf_op jit(solution)/shard_map/hqk,hqd->hkd/dot_general | solution.py:287
  401.3 15.0 %multiply_convert_fusion = bf16[3,1024,2048]{2,1,0:T(8,128)(2,1)} fusion(f32[3,1024]{1,0:T(4,128)} %multiply_reduce_fusion.5, f32[3,1024,2048]{2,1,0:T(8,128)} %get-tuple-element.140, f32[3,1024]{1,0:T(4,128)} %get-tuple-element.139, bf16[3,2048,64]{1,2,0:T(8,128)(2,1)} %bitcast.540, bf16[256,3,64]{0,2,1:T(8,128)(2,1)} %bitcast.113, ...), kind=kOutput, calls=%fused_computation.1 | convolution fusion | flops 832045056 | bytes 38952960 | tf_op jit(solution)/shard_map/hqd,hkd->hqk/dot_general | solution.py:282
  416.3 7.8 %fusion.13 = bf16[3,2048,64]{1,2,0:T(8,128)(2,1)} fusion(bf16[3,1024,64]{1,2,0:T(8,128)(2,1)S(1)} %bitcast.485, bf16[3,1024,2048]{2,1,0:T(8,128)(2,1)} %multiply_convert_fusion), kind=kOutput, calls=%fused_computation.41 | convolution fusion | flops 806092800 | bytes 13762560 | tf_op jit(solution)/shard_map/hqk,hqd->hkd/dot_general | solution.py:286
  424.0 9.4 %fusion.30 = bf16[3,1024,64]{1,2,0:T(8,128)(2,1)} fusion(bf16[3,1024,2048]{2,1,0:T(8,128)(2,1)} %multiply_convert_fusion, bf16[3,2048,64]{1,2,0:T(8,128)(2,1)} %bitcast.545), kind=kOutput, calls=%fused_computation.103 | convolution fusion | flops 805699584 | bytes 13762560 | tf_op jit(solution)/shard_map/hqk,hkd->hqd/dot_general | solution.py:285
  445.6 3.5 multiply_reduce_fusion
  456.6 3.6 copy.115
  479.7 7.5 %collective-permute-done.39 = bf16[2,192,288]{1,2,0:T(8,128)(2,1)S(1)} collective-permute-done((bf16[2,192,288]{1,2,0:T(8,128)(2,1)S(1)}, bf16[2,192,288]{1,2,0:T(8,128)(2,1)S(1)}, u32[]{:S(2)}, u32[]{:S(2)}) %collective-permute-start.39) | collective-permute-done | bytes 221216 | tf_op jit(solution)/shard_map/ppermute | solution.py:52
  489.3 9.6 %collective-permute-done.32 = bf16[256,768]{1,0:T(8,128)(2,1)S(1)} collective-permute-done((bf16[256,768]{1,0:T(8,128)(2,1)S(1)}, bf16[256,768]{1,0:T(8,128)(2,1)S(1)}, u32[]{:S(2)}, u32[]{:S(2)}) %collective-permute-start.32) | collective-permute-done | bytes 393248 | tf_op jit(solution)/shard_map/ppermute | solution.py:42
  538.0 3.6 collective-permute-done.46
  548.4 7.9 %collective-permute-done.50 = bf16[2,192,864]{2,1,0:T(8,128)(2,1)} collective-permute-done((bf16[2,192,864]{2,1,0:T(8,128)(2,1)}, bf16[2,192,864]{2,1,0:T(8,128)(2,1)}, u32[]{:S(2)}, u32[]{:S(2)}) %collective-permute-start.50) | collective-permute-done | bytes 663584 | tf_op jit(solution)/shard_map/ppermute | solution.py:52
  564.2 4.0 collective-permute-done.54
  576.6 6.5 %collective-permute-done.51 = bf16[192,864]{0,1:T(8,128)(2,1)S(1)} collective-permute-done((bf16[192,864]{0,1:T(8,128)(2,1)S(1)}, bf16[192,864]{0,1:T(8,128)(2,1)S(1)}, u32[]{:S(2)}, u32[]{:S(2)}) %collective-permute-start.51) | collective-permute-done | bytes 331808 | tf_op jit(solution)/shard_map/ppermute | solution.py:48
  598.4 7.7 %collective-permute-done.52 = bf16[192,864]{0,1:T(8,128)(2,1)} collective-permute-done((bf16[192,864]{0,1:T(8,128)(2,1)}, bf16[192,864]{0,1:T(8,128)(2,1)}, u32[]{:S(2)}, u32[]{:S(2)}) %collective-permute-start.52) | collective-permute-done | bytes 331808 | tf_op jit(solution)/shard_map/ppermute | solution.py:42
  627.2 3.6 collective-permute-done.59
  637.2 4.9 fusion.141
  (770 shorter events, 427.4 us)
Async XLA Ops:
  2.7 30.0 %collective-permute-start.16 = (bf16[192,864]{1,0:T(8,128)(2,1)S(1)}, bf16[192,864]{1,0:T(8,128)(2,1)S(1)}, u32[]{:S(2)}, u32[]{:S(2)}) collective-permute-start(bf16[192,864]{1,0:T(8,128)(2,1)S(1)} %get-tuple-element.133), channel_id=1, source_target_pairs={{0,2},{1,3},{2,6},{3,7},{6,4},{7,5},{4,0},{5,1},{8,10},{9,11},{10,... | collective-permute-start | bytes 995336 | tf_op jit(solution)/shard_map/ppermute | solution.py:42
  5.8 23.1 %collective-permute-start.13 = (bf16[192,864]{1,0:T(8,128)(2,1)S(1)}, bf16[192,864]{1,0:T(8,128)(2,1)S(1)}, u32[]{:S(2)}, u32[]{:S(2)}) collective-permute-start(bf16[192,864]{1,0:T(8,128)(2,1)S(1)} %get-tuple-element.133), channel_id=1, source_target_pairs={{0,1},{1,0},{2,3},{3,2},{4,5},{5,4},{6,7},{7,6},{8,9},{9,8},{10,11... | collective-permute-start | bytes 995336 | tf_op jit(solution)/shard_map/ppermute | solution.py:48
  8.1 34.0 %collective-permute-start.1 = (bf16[264,768]{1,0:T(8,128)(2,1)}, bf16[264,768]{1,0:T(8,128)(2,1)}, u32[]{:S(2)}, u32[]{:S(2)}) collective-permute-start(bf16[264,768]{1,0:T(8,128)(2,1)} %fusion.55), channel_id=1, source_target_pairs={{0,2},{1,3},{2,6},{3,7},{6,4},{7,5},{4,0},{5,1},{8,10},{9,11},{10,... | collective-permute-start | bytes 1216520 | tf_op jit(solution)/shard_map/ppermute | solution.py:42
  10.7 29.0 %collective-permute-start = (bf16[264,768]{1,0:T(8,128)(2,1)}, bf16[264,768]{1,0:T(8,128)(2,1)}, u32[]{:S(2)}, u32[]{:S(2)}) collective-permute-start(bf16[264,768]{1,0:T(8,128)(2,1)} %fusion.55), channel_id=1, source_target_pairs={{0,1},{1,0},{2,3},{3,2},{4,5},{5,4},{6,7},{7,6},{8,9},{9,8},{10,11... | collective-permute-start | bytes 1216520 | tf_op jit(solution)/shard_map/ppermute | solution.py:48
  29.8 50.6 %collective-permute-start.14 = (bf16[2,192,864]{2,1,0:T(8,128)(2,1)}, bf16[2,192,864]{2,1,0:T(8,128)(2,1)}, u32[]{:S(2)}, u32[]{:S(2)}) collective-permute-start(bf16[2,192,864]{2,1,0:T(8,128)(2,1)} %pad_maximum_fusion.16), channel_id=1, source_target_pairs={{0,16},{8,24},{16,0},{24,8},{1,17},{9,25},{17,1},{25,9},{2,18},{10... | collective-permute-start | bytes 1990664 | tf_op jit(solution)/shard_map/ppermute | solution.py:52
  42.1 25.7 %collective-permute-start.3 = (bf16[264,768]{1,0:T(8,128)(2,1)}, bf16[264,768]{1,0:T(8,128)(2,1)}, u32[]{:S(2)}, u32[]{:S(2)}) collective-permute-start(bf16[264,768]{1,0:T(8,128)(2,1)} %collective-permute-done.1), channel_id=1, source_target_pairs={{0,2},{1,3},{2,6},{3,7},{6,4},{7,5},{4,0},{5,1},{8,10},{9,11},{10,... | collective-permute-start | bytes 1216520 | tf_op jit(solution)/shard_map/ppermute | solution.py:42
  51.1 52.8 %collective-permute-start.18 = (bf16[2,192,864]{2,1,0:T(8,128)(2,1)}, bf16[2,192,864]{2,1,0:T(8,128)(2,1)}, u32[]{:S(2)}, u32[]{:S(2)}) collective-permute-start(bf16[2,192,864]{2,1,0:T(8,128)(2,1)} %pad_maximum_fusion.17), channel_id=1, source_target_pairs={{0,16},{8,24},{16,0},{24,8},{1,17},{9,25},{17,1},{25,9},{2,18},{10... | collective-permute-start | bytes 1990664 | tf_op jit(solution)/shard_map/ppermute | solution.py:52
  52.6 33.6 %collective-permute-start.24 = (bf16[192,864]{1,0:T(8,128)(2,1)}, bf16[192,864]{1,0:T(8,128)(2,1)}, u32[]{:S(2)}, u32[]{:S(2)}) collective-permute-start(bf16[192,864]{1,0:T(8,128)(2,1)} %collective-permute-done.20), channel_id=1, source_target_pairs={{0,2},{1,3},{2,6},{3,7},{6,4},{7,5},{4,0},{5,1},{8,10},{9,11},{10,... | collective-permute-start | bytes 995336 | tf_op jit(solution)/shard_map/ppermute | solution.py:42
  80.5 92.2 %collective-permute-start.22 = (bf16[2,192,864]{2,1,0:T(8,128)(2,1)}, bf16[2,192,864]{2,1,0:T(8,128)(2,1)}, u32[]{:S(2)}, u32[]{:S(2)}) collective-permute-start(bf16[2,192,864]{2,1,0:T(8,128)(2,1)} %pad_maximum_fusion.18), channel_id=1, source_target_pairs={{0,16},{8,24},{16,0},{24,8},{1,17},{9,25},{17,1},{25,9},{2,18},{10... | collective-permute-start | bytes 1990664 | tf_op jit(solution)/shard_map/ppermute | solution.py:52
  86.2 121.2 %collective-permute-start.15 = (bf16[2,384,864]{1,2,0:T(8,128)(2,1)}, bf16[2,384,864]{1,2,0:T(8,128)(2,1)}, u32[]{:S(2)}, u32[]{:S(2)}) collective-permute-start(bf16[2,384,864]{1,2,0:T(8,128)(2,1)} %copy.83), channel_id=1, source_target_pairs={{0,8},{8,0},{16,24},{24,16},{1,9},{9,1},{17,25},{25,17},{2,10},{10... | collective-permute-start | bytes 3981320 | tf_op jit(solution)/shard_map/ppermute | solution.py:52
  87.8 23.2 %collective-permute-start.6 = (bf16[264,768]{1,0:T(8,128)(2,1)}, bf16[264,768]{1,0:T(8,128)(2,1)}, u32[]{:S(2)}, u32[]{:S(2)}) collective-permute-start(bf16[264,768]{1,0:T(8,128)(2,1)} %collective-permute-done.5), channel_id=1, source_target_pairs={{0,1},{1,0},{2,3},{3,2},{4,5},{5,4},{6,7},{7,6},{8,9},{9,8},{10,11... | collective-permute-start | bytes 1216520 | tf_op jit(solution)/shard_map/ppermute | solution.py:48
  100.0 81.2 %collective-permute-start.26 = (bf16[2,192,864]{2,1,0:T(8,128)(2,1)}, bf16[2,192,864]{2,1,0:T(8,128)(2,1)}, u32[]{:S(2)}, u32[]{:S(2)}) collective-permute-start(bf16[2,192,864]{2,1,0:T(8,128)(2,1)} %pad_maximum_fusion.19), channel_id=1, source_target_pairs={{0,16},{8,24},{16,0},{24,8},{1,17},{9,25},{17,1},{25,9},{2,18},{10... | collective-permute-start | bytes 1990664 | tf_op jit(solution)/shard_map/ppermute | solution.py:52
  108.7 103.7 %collective-permute-start.19 = (bf16[2,384,864]{1,2,0:T(8,128)(2,1)}, bf16[2,384,864]{1,2,0:T(8,128)(2,1)}, u32[]{:S(2)}, u32[]{:S(2)}) collective-permute-start(bf16[2,384,864]{1,2,0:T(8,128)(2,1)} %copy.86), channel_id=1, source_target_pairs={{0,8},{8,0},{16,24},{24,16},{1,9},{9,1},{17,25},{25,17},{2,10},{10... | collective-permute-start | bytes 3981320 | tf_op jit(solution)/shard_map/ppermute | solution.py:52
  181.2 22.0 %collective-permute-start.10 = (bf16[256,192]{0,1:T(8,128)(2,1)}, bf16[256,192]{0,1:T(8,128)(2,1)}, u32[]{:S(2)}, u32[]{:S(2)}) collective-permute-start(bf16[256,192]{0,1:T(8,128)(2,1)} %bitcast.556), channel_id=1, source_target_pairs={{0,4},{1,5},{2,0},{3,1},{6,2},{7,3},{4,6},{5,7},{8,12},{9,13},{10,... | collective-permute-start | bytes 294920 | tf_op jit(solution)/shard_map/ppermute | solution.py:42
  186.4 30.5 %collective-permute-start.23 = (bf16[2,384,864]{1,2,0:T(8,128)(2,1)}, bf16[2,384,864]{1,2,0:T(8,128)(2,1)}, u32[]{:S(2)}, u32[]{:S(2)}) collective-permute-start(bf16[2,384,864]{1,2,0:T(8,128)(2,1)} %copy.89), channel_id=1, source_target_pairs={{0,8},{8,0},{16,24},{24,16},{1,9},{9,1},{17,25},{25,17},{2,10},{10... | collective-permute-start | bytes 3981320 | tf_op jit(solution)/shard_map/ppermute | solution.py:52
  186.4 35.0 %collective-permute-start.27 = (bf16[2,384,864]{1,2,0:T(8,128)(2,1)}, bf16[2,384,864]{1,2,0:T(8,128)(2,1)}, u32[]{:S(2)}, u32[]{:S(2)}) collective-permute-start(bf16[2,384,864]{1,2,0:T(8,128)(2,1)} %copy.92), channel_id=1, source_target_pairs={{0,8},{8,0},{16,24},{24,16},{1,9},{9,1},{17,25},{25,17},{2,10},{10... | collective-permute-start | bytes 3981320 | tf_op jit(solution)/shard_map/ppermute | solution.py:52
  349.9 41.7 %collective-permute-start.30 = (bf16[256,192]{0,1:T(8,128)(2,1)}, bf16[256,192]{0,1:T(8,128)(2,1)}, u32[]{:S(2)}, u32[]{:S(2)}) collective-permute-start(bf16[256,192]{0,1:T(8,128)(2,1)} %get-tuple-element.113), channel_id=1, source_target_pairs={{0,4},{1,5},{2,0},{3,1},{6,2},{7,3},{4,6},{5,7},{8,12},{9,13},{10,... | collective-permute-start | bytes 294920 | tf_op jit(solution)/shard_map/ppermute | solution.py:42
  350.7 41.0 %collective-permute-start.29 = (bf16[256,192]{0,1:T(8,128)(2,1)}, bf16[256,192]{0,1:T(8,128)(2,1)}, u32[]{:S(2)}, u32[]{:S(2)}) collective-permute-start(bf16[256,192]{0,1:T(8,128)(2,1)} %get-tuple-element.114), channel_id=1, source_target_pairs={{0,6},{1,7},{2,4},{3,5},{6,0},{7,1},{4,2},{5,3},{8,14},{9,15},{10,... | collective-permute-start | bytes 294920 | tf_op jit(solution)/shard_map/ppermute | solution.py:42
  354.2 37.4 %collective-permute-start.28 = (bf16[256,192]{0,1:T(8,128)(2,1)}, bf16[256,192]{0,1:T(8,128)(2,1)}, u32[]{:S(2)}, u32[]{:S(2)}) collective-permute-start(bf16[256,192]{0,1:T(8,128)(2,1)} %get-tuple-element.115), channel_id=1, source_target_pairs={{0,2},{1,3},{2,6},{3,7},{6,4},{7,5},{4,0},{5,1},{8,10},{9,11},{10,... | collective-permute-start | bytes 294920 | tf_op jit(solution)/shard_map/ppermute | solution.py:42
  371.5 129.4 %collective-permute-start.41 = (bf16[2,384,864]{1,2,0:T(8,128)(2,1)}, bf16[2,384,864]{1,2,0:T(8,128)(2,1)}, u32[]{:S(2)}, u32[]{:S(2)}) collective-permute-start(bf16[2,384,864]{1,2,0:T(8,128)(2,1)} %pad_maximum_fusion.10), channel_id=1, source_target_pairs={{0,8},{8,0},{16,24},{24,16},{1,9},{9,1},{17,25},{25,17},{2,10},{10... | collective-permute-start | bytes 3981320 | tf_op jit(solution)/shard_map/ppermute | solution.py:52
  378.6 129.5 %collective-permute-start.45 = (bf16[2,384,864]{1,2,0:T(8,128)(2,1)}, bf16[2,384,864]{1,2,0:T(8,128)(2,1)}, u32[]{:S(2)}, u32[]{:S(2)}) collective-permute-start(bf16[2,384,864]{1,2,0:T(8,128)(2,1)} %pad_maximum_fusion.9), channel_id=1, source_target_pairs={{0,8},{8,0},{16,24},{24,16},{1,9},{9,1},{17,25},{25,17},{2,10},{10... | collective-permute-start | bytes 3981320 | tf_op jit(solution)/shard_map/ppermute | solution.py:52
  450.6 27.5 %collective-permute-start.31 = (bf16[256,768]{1,0:T(8,128)(2,1)S(1)}, bf16[256,768]{1,0:T(8,128)(2,1)}, u32[]{:S(2)}, u32[]{:S(2)}) collective-permute-start(bf16[256,768]{1,0:T(8,128)(2,1)S(1)} %get-tuple-element.53), channel_id=1, source_target_pairs={{0,1},{1,0},{2,3},{3,2},{4,5},{5,4},{6,7},{7,6},{8,9},{9,8},{10,11... | collective-permute-start | bytes 1179656 | tf_op jit(solution)/shard_map/ppermute | solution.py:48
  476.8 38.6 %collective-permute-start.49 = (bf16[2,384,864]{1,2,0:T(8,128)(2,1)}, bf16[2,384,864]{1,2,0:T(8,128)(2,1)}, u32[]{:S(2)}, u32[]{:S(2)}) collective-permute-start(bf16[2,384,864]{1,2,0:T(8,128)(2,1)} %pad_maximum_fusion.8), channel_id=1, source_target_pairs={{0,8},{8,0},{16,24},{24,16},{1,9},{9,1},{17,25},{25,17},{2,10},{10... | collective-permute-start | bytes 3981320 | tf_op jit(solution)/shard_map/ppermute | solution.py:52
  488.6 35.0 %collective-permute-start.53 = (bf16[2,384,864]{1,2,0:T(8,128)(2,1)}, bf16[2,384,864]{1,2,0:T(8,128)(2,1)}, u32[]{:S(2)}, u32[]{:S(2)}) collective-permute-start(bf16[2,384,864]{1,2,0:T(8,128)(2,1)} %pad_maximum_fusion.7), channel_id=1, source_target_pairs={{0,8},{8,0},{16,24},{24,16},{1,9},{9,1},{17,25},{25,17},{2,10},{10... | collective-permute-start | bytes 3981320 | tf_op jit(solution)/shard_map/ppermute | solution.py:52
  498.8 92.9 %collective-permute-start.35 = (bf16[256,768]{1,0:T(8,128)(2,1)}, bf16[256,768]{1,0:T(8,128)(2,1)}, u32[]{:S(2)}, u32[]{:S(2)}) collective-permute-start(bf16[256,768]{1,0:T(8,128)(2,1)} %get-tuple-element.51), channel_id=1, source_target_pairs={{0,1},{1,0},{2,3},{3,2},{4,5},{5,4},{6,7},{7,6},{8,9},{9,8},{10,11... | collective-permute-start | bytes 1179656 | tf_op jit(solution)/shard_map/ppermute | solution.py:48
  500.9 118.8 %collective-permute-start.37 = (bf16[256,768]{1,0:T(8,128)(2,1)}, bf16[256,768]{1,0:T(8,128)(2,1)}, u32[]{:S(2)}, u32[]{:S(2)}) collective-permute-start(bf16[256,768]{1,0:T(8,128)(2,1)} %get-tuple-element.50), channel_id=1, source_target_pairs={{0,1},{1,0},{2,3},{3,2},{4,5},{5,4},{6,7},{7,6},{8,9},{9,8},{10,11... | collective-permute-start | bytes 1179656 | tf_op jit(solution)/shard_map/ppermute | solution.py:48
  508.1 22.6 %collective-permute-start.42 = (bf16[2,192,864]{2,1,0:T(8,128)(2,1)}, bf16[2,192,864]{2,1,0:T(8,128)(2,1)}, u32[]{:S(2)}, u32[]{:S(2)}) collective-permute-start(bf16[2,192,864]{2,1,0:T(8,128)(2,1)} %copy.117), channel_id=1, source_target_pairs={{0,16},{8,24},{16,0},{24,8},{1,17},{9,25},{17,1},{25,9},{2,18},{10... | collective-permute-start | bytes 1990664 | tf_op jit(solution)/shard_map/ppermute | solution.py:52
  515.4 26.2 %collective-permute-start.46 = (bf16[2,192,864]{2,1,0:T(8,128)(2,1)}, bf16[2,192,864]{2,1,0:T(8,128)(2,1)}, u32[]{:S(2)}, u32[]{:S(2)}) collective-permute-start(bf16[2,192,864]{2,1,0:T(8,128)(2,1)} %copy.119), channel_id=1, source_target_pairs={{0,16},{8,24},{16,0},{24,8},{1,17},{9,25},{17,1},{25,9},{2,18},{10... | collective-permute-start | bytes 1990664 | tf_op jit(solution)/shard_map/ppermute | solution.py:52
  523.6 32.8 %collective-permute-start.50 = (bf16[2,192,864]{2,1,0:T(8,128)(2,1)}, bf16[2,192,864]{2,1,0:T(8,128)(2,1)}, u32[]{:S(2)}, u32[]{:S(2)}) collective-permute-start(bf16[2,192,864]{2,1,0:T(8,128)(2,1)} %copy.121), channel_id=1, source_target_pairs={{0,16},{8,24},{16,0},{24,8},{1,17},{9,25},{17,1},{25,9},{2,18},{10... | collective-permute-start | bytes 1990664 | tf_op jit(solution)/shard_map/ppermute | solution.py:52
  530.8 37.5 %collective-permute-start.54 = (bf16[2,192,864]{2,1,0:T(8,128)(2,1)}, bf16[2,192,864]{2,1,0:T(8,128)(2,1)}, u32[]{:S(2)}, u32[]{:S(2)}) collective-permute-start(bf16[2,192,864]{2,1,0:T(8,128)(2,1)} %copy.123), channel_id=1, source_target_pairs={{0,16},{8,24},{16,0},{24,8},{1,17},{9,25},{17,1},{25,9},{2,18},{10... | collective-permute-start | bytes 1990664 | tf_op jit(solution)/shard_map/ppermute | solution.py:52
  591.7 24.9 %collective-permute-start.65 = (f32[4,768]{1,0:T(4,128)S(1)}, f32[4,768]{1,0:T(4,128)}, u32[]{:S(2)}, u32[]{:S(2)}) collective-permute-start(f32[4,768]{1,0:T(4,128)S(1)} %add.609), channel_id=1, source_target_pairs={{0,4},{1,5},{2,6},{3,7},{4,0},{5,1},{6,2},{7,3},{8,12},{9,13},{10,... | collective-permute-start | bytes 36872 | tf_op jit(solution)/shard_map/ppermute | solution.py:52
  598.4 21.4 %collective-permute-start.36 = (bf16[256,768]{1,0:T(8,128)(2,1)}, bf16[256,768]{1,0:T(8,128)(2,1)}, u32[]{:S(2)}, u32[]{:S(2)}) collective-permute-start(bf16[256,768]{1,0:T(8,128)(2,1)} %add_convert_fusion.12), channel_id=1, source_target_pairs={{0,2},{1,3},{2,6},{3,7},{6,4},{7,5},{4,0},{5,1},{8,10},{9,11},{10,... | collective-permute-start | bytes 1179656 | tf_op jit(solution)/shard_map/ppermute | solution.py:42
  (212 other events, 1258.6 us)

commit v2 on v1

--- a/solution.py
+++ b/solution.py
@@ -4,6 +4,8 @@
 import jax
 import jax.numpy as jnp
 from jax import lax
+from jax.experimental import pallas as pl
+from jax.experimental.pallas import tpu as pltpu
 from jax.sharding import PartitionSpec as P
 
 D = 768
@@ -138,7 +140,14 @@
     return (params_new, first_new, second_new)
 
 
-def local(
+def relative(dp, absolute, order):
+    index = jnp.int32(0)
+    for at, offset in enumerate(order):
+        index = jnp.where((dp ^ absolute) == offset, at, index)
+    return index
+
+
+def step_general(
     patches,
     cotangent,
     input_views,
@@ -342,18 +351,685 @@
     )
 
 
-def relative(dp, absolute, order):
-    index = jnp.int32(0)
-    for at, offset in enumerate(order):
-        index = jnp.where((dp ^ absolute) == offset, at, index)
-    return index
+HALF = 48
+ANY = pl.BlockSpec(memory_space=pl.ANY)
+SMEM = pl.BlockSpec(memory_space=pltpu.SMEM)
+VMEM_LIMIT = 56 << 20
+
+
+def call(body, name, ins, outs, operands, scratch=(), aliases=None):
+    return pl.pallas_call(
+        body,
+        name=name,
+        out_shape=outs,
+        in_specs=ins,
+        out_specs=jax.tree.map(lambda _: pl.BlockSpec(memory_space=pltpu.VMEM), outs),
+        scratch_shapes=list(scratch),
+        input_output_aliases=aliases or {},
+        compiler_params=pltpu.CompilerParams(vmem_limit_bytes=VMEM_LIMIT),
+    )(*operands)
+
+
+VM = pl.BlockSpec(memory_space=pltpu.VMEM)
+
+
+def shape(dims, dtype):
+    return jax.ShapeDtypeStruct(dims, dtype)
+
+
+def run_copies(copies):
+    for c in copies:
+        c.start()
+    for c in copies:
+        c.wait()
+
+
+def place_qkv(own, x_place, y_place, core, pieces):
+    def body(at, pieces_ref, out_ref, sems):
+        x, y, c = at[0], at[1], at[2]
+        copies = []
+        for block in range(3):
+            for xa in range(2):
+                for half in range(2):
+                    for ya in range(2):
+                        source = ((x ^ xa) * 2 + (y ^ ya)) * 2 + (c ^ half)
+                        row = block * GROUP_WIDTH + (xa * 2 + half) * HALF
+                        copies.append(
+                            pltpu.make_async_copy(
+                                pieces_ref.at[source, pl.ds(block * HALF, HALF), :],
+                                out_ref.at[pl.ds(row, HALF), pl.ds(ya * 384, 384)],
+                                sems.at[len(copies)],
+                            )
+                        )
+        run_copies(copies)
+
+    at = jnp.stack([x_place, y_place, core]).astype(jnp.int32)
+    return call(
+        body, "place_qkv", [SMEM, ANY], shape((3 * GROUP_WIDTH, D), bf16), (at, pieces), [pltpu.SemaphoreType.DMA((24,))]
+    )
+
+
+def place_out(at, own_half, other_half):
+    def body(at_ref, own_ref, other_ref, out_ref, sems):
+        x, y, c, place = at_ref[0], at_ref[1], at_ref[2], at_ref[3]
+        copies = []
+        for k in range(4):
+            quarter = gray((place - k) & 3)
+            for j in range(2):
+                for r in range(2):
+                    for h, ref in ((0, own_ref), (1, other_ref)):
+                        row = (quarter * 2 + (x ^ j)) * 96 + (c ^ h) * HALF
+                        copies.append(
+                            pltpu.make_async_copy(
+                                ref.at[(k * 2 + j) * 2 + r],
+                                out_ref.at[
+                                    pl.ds(pl.multiple_of(row, 16), HALF),
+                                    pl.ds(pl.multiple_of((y ^ r) * 384, 128), 384),
+                                ],
+                                sems.at[len(copies)],
+                            )
+                        )
+        run_copies(copies)
+
+    return call(
+        body,
+        "place_out",
+        [SMEM, ANY, ANY],
+        shape((D, D), bf16),
+        (at, own_half, other_half),
+        [pltpu.SemaphoreType.DMA((32,))],
+    )
+
+
+def normalize(values):
+    centre = jnp.mean(values, axis=-1, keepdims=True)
+    shifted = values - centre
+    inverse = lax.rsqrt(jnp.mean(shifted * shifted, axis=-1, keepdims=True) + layer_eps)
+    return shifted * inverse, inverse
+
+
+def lane_index(dims):
+    return lax.broadcasted_iota(jnp.int32, dims, len(dims) - 1)
+
+
+def project(first, second, w_t, norms):
+    def body(a_ref, b_ref, w_ref, norm_ref, act_ref, normal_ref, q_ref, k_ref, v_ref, wide_ref):
+        wide_ref[...] = jnp.zeros_like(wide_ref)
+        for h in range(9):
+            wide_ref[h * 128 : h * 128 + 64, :] = w_ref[h * 64 : h * 64 + 64, :]
+        gain, shift = norm_ref[0:1, :], norm_ref[1:2, :]
+        for piece, ref in enumerate((a_ref, b_ref)):
+            at = slice(piece * 256, piece * 256 + 256)
+            normal, _ = normalize(ref[0:256, :].astype(f32))
+            act = (normal * gain + shift).astype(bf16)
+            normal_ref[at, :] = normal.astype(bf16)
+            act_ref[at, :] = act
+            flags = ref[256:257, 0:256].astype(f32)
+            mask = jnp.where(flags > 0, 0.0, masked_score)
+            mask = jnp.transpose(jnp.broadcast_to(mask, (128, 256)))
+            lanes = lane_index((256, 128))
+            for h in range(3):
+                if piece == 0:
+                    q = mm_nt(act, wide_ref[h * 128 : h * 128 + 128, :]).astype(bf16).astype(f32)
+                    q = jnp.where(lanes == 64, 1.0, q * (1.0 / math.sqrt(HEAD_DIM)))
+                    q_ref[h] = q.astype(bf16)
+                k = mm_nt(act, wide_ref[(3 + h) * 128 : (4 + h) * 128, :])
+                k = jnp.where(lanes == 64, mask, k)
+                k_ref[h, at, :] = jnp.where((lanes > 64) & (lanes < 68), 1.0, k).astype(bf16)
+                v = mm_nt(act, wide_ref[(6 + h) * 128 : (7 + h) * 128, :])
+                v_ref[h, at, :] = jnp.where((lanes > 63) & (lanes < 67), 1.0, v).astype(bf16)
+
+    outs = [
+        shape((512, D), bf16),
+        shape((512, D), bf16),
+        shape((3, 256, 128), bf16),
+        shape((3, 512, 128), bf16),
+        shape((3, 512, 128), bf16),
+    ]
+    return call(body, "norm_project", [VM] * 4, outs, (first, second, w_t, norms), [pltpu.VMEM((1152, D), bf16)])
+
+
+def in_three(value):
+    high = value.astype(bf16).astype(f32)
+    rest = value - high
+    mid = rest.astype(bf16).astype(f32)
+    return high, mid, rest - mid
+
+
+def with_parts(base, lanes, first, value):
+    for i, part in enumerate(in_three(value)):
+        base = jnp.where(lanes == first + i, part, base)
+    return base
+
+
+def join_heads(parts):
+    return jnp.concatenate([p[:, :HEAD_DIM] for p in parts], axis=1)
+
+
+def attend(seen, qs, ks, vs):
+    def body(seen_ref, *refs):
+        q_refs, k_refs, v_refs = refs[0:4], refs[4:8], refs[8:12]
+        low_refs, full_ref, back_refs = refs[12:16], refs[16], refs[17:21]
+        top_ref, sum_ref = refs[21:23]
+        lanes = lane_index((256, 128))
+
+        def head(h, _):
+            for i in range(4):
+                q = q_refs[i][h]
+                s = mm_nt(q, k_refs[i][h])
+                top = jnp.max(s, axis=-1, keepdims=True)
+                top_ref[...] = jnp.broadcast_to(top, (256, 128))
+                sum_ref[...] = mm(jnp.exp(s - top).astype(bf16), v_refs[i][h])
+                for c in range(4):
+                    if c == i:
+                        continue
+
+                    @pl.when(seen_ref[i * 4 + c] > 0)
+                    def _():
+                        s = mm_nt(q, k_refs[c][h])
+                        old = top_ref[:, 0:1]
+                        top = jnp.maximum(old, jnp.max(s, axis=-1, keepdims=True))
+                        top_ref[...] = jnp.broadcast_to(top, (256, 128))
+                        p = jnp.exp(s - top).astype(bf16)
+                        sum_ref[...] = sum_ref[...] * jnp.exp(old - top) + mm(p, v_refs[c][h])
+
+                mixed = sum_ref[...]
+                norm = mixed[:, HEAD_DIM : HEAD_DIM + 1]
+                full_ref[h, i] = mixed / norm
+                logsum = top_ref[:, 0:1] + jnp.log(norm)
+                back_refs[i][h] = with_parts(q.astype(f32), lanes, 65, -logsum).astype(bf16)
+            return 0
+
+        lax.fori_loop(0, 3, head, 0)
+        for i in range(4):
+            low_refs[i][...] = join_heads([full_ref[h, i] for h in range(3)]).astype(bf16)
+
+    outs = (
+        [shape((256, GROUP_WIDTH), bf16)] * 4 + [shape((3, 4, 256, 128), f32)] + [shape((3, 256, 128), bf16)] * 4
+    )
+    got = call(
+        body,
+        "attend",
+        [SMEM] + [VM] * 12,
+        outs,
+        (seen, *qs, *ks, *vs),
+        [pltpu.VMEM((256, 128), f32), pltpu.VMEM((256, 128), f32)],
+    )
+    return got[0:4], got[4], got[5:9]
+
+
+def attend_back(seen, qs, ks, vs, full, grads):
+    def body(seen_ref, *refs):
+        q_refs, k_refs, v_refs, full_ref, g_refs = refs[0:4], refs[4:8], refs[8:12], refs[12], refs[13:17]
+        dq_refs, dk_refs, dv_refs = refs[17:21], refs[21:25], refs[25:29]
+        g_ref, dq_ref, dk_ref, dv_ref = refs[29:33]
+        lanes = lane_index((256, 128))
+        for i in range(4):
+            for h in range(3):
+                g = g_refs[i][:, h * 64 : h * 64 + 64].astype(f32)
+                delta = jnp.sum(g * full_ref[h, i][:, :64], axis=-1, keepdims=True)
+                g = jnp.concatenate([g, jnp.zeros((256, 64), f32)], axis=1)
+                g_ref[h, i] = with_parts(g, lanes, 64, -delta).astype(bf16)
+        dq_ref[...] = jnp.zeros_like(dq_ref)
+        dk_ref[...] = jnp.zeros_like(dk_ref)
+        dv_ref[...] = jnp.zeros_like(dv_ref)
+
+        def head(h, _):
+            for c in range(4):
+                k, v = k_refs[c][h], v_refs[c][h]
+                for i in range(4):
+
+                    @pl.when(seen_ref[i * 4 + c] > 0)
+                    def _():
+                        q, g = q_refs[i][h], g_ref[h, i]
+                        p = jnp.exp(mm_nt(k, q))
+                        ds = (p * mm_nt(v, g)).astype(bf16)
+                        dv_ref[h, c] += mm(p.astype(bf16), g)
+                        dk_ref[h, c] += mm(ds, q)
+                        dq_ref[h, i] += mm_tn(ds, k)
+
+            return 0
+
+        lax.fori_loop(0, 3, head, 0)
+        for i in range(4):
+            dq_refs[i][...] = (join_heads([dq_ref[h, i] for h in range(3)]) * (1.0 / math.sqrt(HEAD_DIM))).astype(bf16)
+            dk_refs[i][...] = join_heads([dk_ref[h, i] for h in range(3)]).astype(bf16)
+            dv_refs[i][...] = join_heads([dv_ref[h, i] for h in range(3)]).astype(bf16)
+
+    outs = [shape((256, GROUP_WIDTH), bf16)] * 4 + [shape((512, GROUP_WIDTH), bf16)] * 8
+    got = call(
+        body,
+        "attend_back",
+        [SMEM] + [VM] * 17,
+        outs,
+        (seen, *qs, *ks, *vs, full, *grads),
+        [
+            pltpu.VMEM((3, 4, 256, 128), bf16),
+            pltpu.VMEM((3, 4, 256, 128), f32),
+            pltpu.VMEM((3, 4, 512, 128), f32),
+            pltpu.VMEM((3, 4, 512, 128), f32),
+        ],
+    )
+    return got[0:4], got[4:8], got[8:12]
+
+
+def project_back(at, acts, normals, dqs, dks, dvs, w_t):
+    def body(at_ref, *refs):
+        act_refs, normal_refs, dq_refs, dk_refs, dv_refs, w_ref = (
+            refs[0:4],
+            refs[4:8],
+            refs[8:12],
+            refs[12:16],
+            refs[16:20],
+            refs[20],
+        )
+        keep_refs, send_refs, w_keep_ref, w_send_ref, norm_ref, dw_ref = refs[21:25], refs[25:29], *refs[29:33]
+        gains, shifts = jnp.zeros((1, D), f32), jnp.zeros((1, D), f32)
+        for i in range(4):
+            act = act_refs[i][...]
+            for b, (ref, rows) in enumerate(((dq_refs[i], 256), (dk_refs[i], 512), (dv_refs[i], 512))):
+                part = mm_tn(ref[...], act[:rows])
+                at_rows = slice(b * GROUP_WIDTH, (b + 1) * GROUP_WIDTH)
+                dw_ref[at_rows, :] = part if i == 0 else dw_ref[at_rows, :] + part
+            for j, out_ref in enumerate((keep_refs[i], send_refs[i])):
+                r = slice(j * 256, j * 256 + 256)
+                one = mm(dk_refs[i][r, :], w_ref[192:384, :]) + mm(dv_refs[i][r, :], w_ref[384:576, :])
+                if j == 0:
+                    one = one + mm(dq_refs[i][...], w_ref[0:192, :])
+                gains = gains + jnp.sum(one * normal_refs[i][r, :].astype(f32), axis=0, keepdims=True)
+                shifts = shifts + jnp.sum(one, axis=0, keepdims=True)
+                out_ref[...] = one.astype(bf16)
+        norm_ref[...] = jnp.concatenate([gains, shifts, jnp.zeros((6, D), f32)], axis=0)
+        x, c = at_ref[0], at_ref[2]
+        for b in range(3):
+            for xa in range(2):
+                for half in range(2):
+                    row = b * GROUP_WIDTH + (xa * 2 + half) * HALF
+                    block = dw_ref[row : row + HALF, :].astype(bf16)
+
+                    @pl.when(c == half)
+                    def _():
+                        w_keep_ref[(x ^ xa) * 3 + b] = block
+
+                    @pl.when(c != half)
+                    def _():
+                        w_send_ref[(x ^ xa) * 3 + b] = block
+
+    outs = (
+        [shape((256, D), bf16)] * 8 + [shape((6, HALF, D), bf16)] * 2 + [shape((8, D), f32)]
+    )
+    got = call(
+        body,
+        "project_back",
+        [SMEM] + [VM] * 21,
+        outs,
+        (at, *acts, *normals, *dqs, *dks, *dvs, w_t),
+        [pltpu.VMEM((3 * GROUP_WIDTH, D), f32)],
+    )
+    return got[0:4], got[4:8], got[8], got[9], got[10]
+
+
+def out_norm(at, patches, mixed, w_out, norms):
+    def body(at_ref, x_ref, m0, m1, m2, m3, w_ref, norm_ref, two_ref, resid_ref, normal_ref, inverse_ref, three_ref):
+        place = at_ref[3]
+        parts = [m[...].astype(f32) for m in (m0, m1, m2, m3)]
+        groups = []
+        for a in range(4):
+            steps = (gray(a) - place) & 3
+            part = parts[0]
+            for k in (1, 2, 3):
+                part = jnp.where(steps == k, parts[k], part)
+            groups.append(part)
+        two = jnp.concatenate(groups, axis=1).astype(bf16)
+        two_ref[...] = two
+        resid = x_ref[...].astype(f32) + mm_nt(two, w_ref[...])
+        resid_ref[...] = resid
+        normal, inverse = normalize(resid)
+        normal_ref[...] = normal
+        inverse_ref[...] = jnp.broadcast_to(inverse, (256, 128))
+        three_ref[...] = (normal * norm_ref[2:3, :] + norm_ref[3:4, :]).astype(bf16)
+
+    outs = [
+        shape((256, D), bf16),
+        shape((256, D), f32),
+        shape((256, D), f32),
+        shape((256, 128), f32),
+        shape((256, D), bf16),
+    ]
+    return call(body, "out_norm", [SMEM] + [VM] * 7, outs, (at, patches, *mixed, w_out, norms))
+
+
+def mlp(at, acts, cots, weights, carried, last):
+    count = len(weights)
+
+    def body(at_ref, *refs):
+        a_refs, c_refs = refs[0:2], refs[2:4]
+        w_refs = refs[4 : 4 + 4 * count]
+        at_in = 4 + 4 * count
+        carried_refs = refs[at_in : at_in + len(carried)]
+        outs = refs[at_in + len(carried) :]
+        out_ref, three_ref = outs[0:2]
+        keep_refs, send_refs = outs[2 : 2 + count], outs[2 + count : 2 + 2 * count]
+        act_ref, cot_ref, w_ref, out_acc, three_acc, sems = outs[2 + 2 * count + (2 if last else 0) :]
+        y = at_ref[1]
+        own_lanes = pl.ds(pl.multiple_of(y * 384, 128), 384)
+        other_lanes = pl.ds(pl.multiple_of((1 - y) * 384, 128), 384)
+        copies = []
+        for n in range(count):
+            group = []
+            for r, lanes in enumerate((own_lanes, other_lanes)):
+                for j in range(2):
+                    for u in range(2):
+                        group.append(
+                            pltpu.make_async_copy(
+                                w_refs[4 * n + 2 * r + j].at[pl.ds(u * 192, 192), :],
+                                w_ref.at[n, u, pl.ds(j * 192, 192), lanes],
+                                sems.at[n, len(group)],
+                            )
+                        )
+            copies.append(group)
+            for c in group:
+                c.start()
+        for i in range(2):
+            act_ref[i * 256 : i * 256 + 256, :] = a_refs[i][...]
+            cot_ref[i * 256 : i * 256 + 256, :] = c_refs[i][...]
+        for n in range(count):
+            for c in copies[n]:
+                c.wait()
+            act, cot = act_ref[...], cot_ref[...]
+            up, down = w_ref[n, 0], w_ref[n, 1]
+            widened = mm_nt(act, up)
+            inner = 0.5 * (1.0 + lax.erf(widened * (1.0 / math.sqrt(2.0))))
+            slope = inner + widened * jnp.exp(-0.5 * widened * widened) * (1.0 / math.sqrt(2.0 * math.pi))
+            hidden = (widened * inner).astype(bf16)
+            grad_wide = (mm_nt(cot, down) * slope).astype(bf16)
+            out = mm(hidden, down)
+            three = mm(grad_wide, up)
+            if n == 0 and not carried:
+                out_acc[...] = out
+                three_acc[...] = three
+            elif n == 0:
+                out_acc[...] = carried_refs[0][...] + out
+                three_acc[...] = carried_refs[1][...] + three
+            else:
+                out_acc[...] += out
+                three_acc[...] += three
+            for lanes, ref in ((own_lanes, keep_refs[n]), (other_lanes, send_refs[n])):
+                grad_up = mm_tn(grad_wide, act_ref[:, lanes]).astype(bf16)
+                grad_down = mm_tn(hidden, cot_ref[:, lanes]).astype(bf16)
+                for j in range(2):
+                    ref[j, 0:192, :] = grad_up[j * 192 : j * 192 + 192]
+                    ref[j, 192:384, :] = grad_down[j * 192 : j * 192 + 192]
+        if last:
+            out_ref[...] = out_acc[0:256, :]
+            three_ref[...] = three_acc[0:256, :]
+            outs[2 + 2 * count][...] = out_acc[256:512, :].astype(bf16)
+            outs[3 + 2 * count][...] = three_acc[256:512, :].astype(bf16)
+        else:
+            out_ref[...] = out_acc[...]
+            three_ref[...] = three_acc[...]
+
+    rows = 256 if last else 512
+    outs = [shape((rows, D), f32)] * 2 + [shape((2, 384, 384), bf16)] * (2 * count)
+    if last:
+        outs = outs + [shape((256, D), bf16)] * 2
+    flat = [w for group in weights for w in group]
+    return call(
+        body,
+        "mlp",
+        [SMEM] + [VM] * 4 + [ANY] * len(flat) + [VM] * len(carried),
+        outs,
+        (at, *acts, *cots, *flat, *carried),
+        [
+            pltpu.VMEM((512, D), bf16),
+            pltpu.VMEM((512, D), bf16),
+            pltpu.VMEM((count, 2, 384, D), bf16),
+            pltpu.VMEM((512, D), f32),
+            pltpu.VMEM((512, D), f32),
+            pltpu.SemaphoreType.DMA((count, 8)),
+        ],
+    )
+
+
+def norm_out_back(at, three, three_there, cotangent, normal, inverse, two, w_out, norms):
+    def body(at_ref, t_ref, s_ref, c_ref, n_ref, i_ref, two_ref, w_ref, norm_ref, *outs):
+        resid_ref, sums_ref = outs[0:2]
+        g_refs, keep_ref, send_ref, dw_ref = outs[2:6], outs[6], outs[7], outs[8]
+        x, c, place = at_ref[0], at_ref[2], at_ref[3]
+        grad = t_ref[...] + s_ref[...].astype(f32)
+        normal = n_ref[...]
+        sums_ref[...] = jnp.concatenate(
+            [jnp.sum(grad * normal, axis=0, keepdims=True), jnp.sum(grad, axis=0, keepdims=True), jnp.zeros((6, D), f32)],
+            axis=0,
+        )
+        resid = c_ref[...].astype(f32) + layer_back(grad, normal, i_ref[:, 0:1], norm_ref[2:3, :])
+        resid_ref[...] = resid
+        low = resid.astype(bf16)
+        back = mm(low, w_ref[...])
+        groups = [back[:, a * GROUP_WIDTH : (a + 1) * GROUP_WIDTH] for a in range(4)]
+        for k in range(4):
+            ahead = gray((place + k) & 3)
+            part = groups[0]
+            for a in (1, 2, 3):
+                part = jnp.where(ahead == a, groups[a], part)
+            g_refs[k][...] = part.astype(bf16)
+        dw_ref[...] = mm_tn(low, two_ref[...])
+        for q in range(4):
+            for xa in range(2):
+                slot = ((place - gray(q)) & 3) * 2 + (x ^ xa)
+                for half in range(2):
+                    row = (q * 2 + xa) * 96 + half * HALF
+                    block = dw_ref[row : row + HALF, :].astype(bf16)
+
+                    @pl.when(c == half)
+                    def _():
+                        keep_ref[slot] = block
+
+                    @pl.when(c != half)
+                    def _():
+                        send_ref[slot] = block
+
+    outs = (
+        [shape((256, D), f32), shape((8, D), f32)]
+        + [shape((256, GROUP_WIDTH), bf16)] * 4
+        + [shape((8, HALF, D), bf16)] * 2
+    )
+    got = call(
+        body,
+        "norm_out_back",
+        [SMEM] + [VM] * 8,
+        outs,
+        (at, three, three_there, cotangent, normal, inverse, two, w_out, norms),
+        [pltpu.VMEM((D, D), f32)],
+    )
+    return got[0], got[1], got[2:6], got[6], got[7]
+
+
+def add_low(a, b):
+    return (a.astype(f32) + b.astype(f32)).astype(bf16)
+
+
+def step_small(
+    patches,
+    cotangent,
+    input_views,
+    token_live,
+    master,
+    moment_one,
+    moment_two,
+    norm_params,
+    norm_moment_one,
+    norm_moment_two,
+):
+    tokens = patches.shape[0]
+    rows, blocks, cols = master.shape
+    dp = lax.axis_index("dp")
+    seq = lax.axis_index("seq")
+    quarter, x_place = seq // 2, seq % 2
+    y_place, core = dp // 2, dp % 2
+    place = gray(quarter)
+    at = jnp.stack([x_place, y_place, core, place]).astype(jnp.int32)
+
+    def to_core(value):
+        return swap(value, "dp", 1)
+
+    def to_y(value):
+        return swap(value, "dp", 2)
+
+    def to_x(value):
+        return swap(value, "seq", 1)
+
+    def by_core(first, second):
+        return jnp.where(core == 0, first, second), jnp.where(core == 0, second, first)
+
+    flags = jnp.pad(token_live.astype(bf16)[None, :], ((0, 7), (0, D - tokens)))
+    ring = [jnp.concatenate([patches, flags], axis=0)]
+    for _ in range(3):
+        ring.append(hop_quarter(ring[-1], 1))
+    beside = [to_x(piece) for piece in ring]
+    cot_there = to_core(cotangent)
+
+    low_t = jnp.transpose(master.astype(bf16), (1, 2, 0))
+    halves = [
+        jnp.concatenate(
+            [
+                low_t[4 + 2 * h : 6 + 2 * h].reshape(2 * cols, rows),
+                low_t[8 + 2 * h : 10 + 2 * h].reshape(2 * cols, rows),
+                low_t[3, h * HALF : (h + 1) * HALF],
+                low_t[0:3, h * HALF : (h + 1) * HALF].reshape(3 * HALF, rows),
+            ],
+            axis=0,
+        )
+        for h in range(2)
+    ]
+    own, other = by_core(*halves)
+    there = to_core(other)
+    both = jnp.concatenate(by_core(own, there), axis=1)
+    far = [both[:432]]
+    near = both[432:]
+    near = [near, to_x(near)]
+    near = jnp.stack([near[0], to_y(near[0]), near[1], to_y(near[1])])
+    near_there = to_core(near)
+    near = jnp.stack([near, near_there], axis=1).reshape(8, 3 * HALF, 2 * rows)
+    w_qkv = place_qkv(None, x_place, y_place, core, near)
+
+    for _ in range(3):
+        far.append(hop_quarter(far[-1], 1))
+    far_x = [to_x(piece) for piece in far]
+    far_y = [to_y(piece) for piece in far]
+    far_xy = [to_y(piece) for piece in far_x]
+    w_mlp = [(far[k], far_x[k], far_y[k], far_xy[k]) for k in range(4)]
+    out_own = jnp.stack([p[384:] for k in range(4) for p in (far[k], far_y[k], far_x[k], far_xy[k])])
+    w_out = place_out(at, out_own, to_core(out_own))
+
+    got = [project(ring[k], beside[k], w_qkv, norm_params) for k in range(4)]
+    acts, normals, qs, ks, vs = zip(*got)
+    inputs_seen = input_views[0]
+    views = jnp.stack([gray((place - k) & 3) * 2 * tokens // VIEW for k in range(4)])
+    seen = (views[None, :] < inputs_seen) | (views[None, :] == views[:, None])
+    seen = seen.astype(jnp.int32).reshape(16)
+    mixed, full, qs_back = attend(seen, qs, ks, vs)
+    mixed = [mixed[0]] + [hop_quarter(mixed[4 - k], k) for k in (3, 2, 1)]
+
+    two, resid, normal_two, inverse_two, act_three = out_norm(at, patches, mixed, w_out, norm_params)
+
+    acts3 = (act_three, to_core(act_three))
+    cots = (cotangent, cot_there)
+    first = mlp(at, acts3, cots, [w_mlp[1], w_mlp[2]], (), False)
+    second = mlp(at, acts3, cots, [w_mlp[3], w_mlp[0]], first[0:2], True)
+    out_mine, three_mine = second[0:2]
+    out_send, three_send = second[6:8]
+    keep = {1: first[2], 2: first[3], 3: second[2], 0: second[3]}
+    send = {1: first[4], 2: first[5], 3: second[4], 0: second[5]}
+    block_out = (resid + out_mine + to_core(out_send).astype(f32)).astype(bf16)
+
+    grad_resid, sums_two, parts, w_out_keep, w_out_send = norm_out_back(
+        at, three_mine, to_core(three_send), cotangent, normal_two, inverse_two, two, w_out, norm_params
+    )
+    grads = [parts[0]] + [hop_quarter(parts[k], k) for k in (1, 2, 3)]
+    dqs, dks, dvs = attend_back(seen, qs_back, ks, vs, full, grads)
+    one_keep, one_send, near_keep, near_send, sums_one = project_back(at, acts, normals, dqs, dks, dvs, w_qkv)
+
+    one = [add_low(one_keep[k], to_x(one_send[k])) for k in range(4)]
+    grad_one = reduce_ring(one)
+    normal_one, inverse_one = layer_stats(patches.astype(f32))
+    patches_grad = grad_resid + layer_back(grad_one, normal_one, inverse_one, norm_params[0])
+    param_grad = total(jnp.concatenate([sums_one[0:2], sums_two[0:2]], axis=0))
+
+    def own_y(value):
+        return lax.dynamic_slice_in_dim(value, y_place * 384, 384, value.ndim - 1)
+
+    def other_y(value):
+        return lax.dynamic_slice_in_dim(value, (1 - y_place) * 384, 384, value.ndim - 1)
+
+    out_sum = add_low(w_out_keep, to_core(w_out_send))
+    out_sum = add_low(own_y(out_sum), to_y(other_y(out_sum)))
+    slots = []
+    for k in range(4):
+        pair = add_low(keep[k], to_y(send[k]))
+        stay = jnp.concatenate([pair[0], out_sum[2 * k]], axis=0)
+        leave = jnp.concatenate([pair[1], out_sum[2 * k + 1]], axis=0)
+        slots.append(add_low(stay, to_x(leave)))
+    far_sum = reduce_ring(slots)
+
+    near_sum = add_low(near_keep, to_core(near_send))
+    near_sum = add_low(own_y(near_sum), to_y(other_y(near_sum)))
+    near_sum = near_sum[0:3].astype(f32) + to_x(near_sum[3:6]).astype(f32)
+
+    grads_t = jnp.concatenate([far_sum, near_sum.reshape(3 * HALF, 2 * rows)], axis=0)
+    squares = jnp.sum(grads_t * grads_t)
+    squares = total(jnp.full((8, 128), squares, f32))[0, 0] + jnp.sum(param_grad * param_grad)
+    grad_norm = jnp.sqrt(squares)
+    clip = 1.0 / jnp.maximum(grad_norm, 1.0)
+    own, other = by_core(grads_t[:, :rows], grads_t[:, rows:])
+    there = to_core(other.astype(bf16)).astype(f32)
+    first, second = by_core(own, there)
+
+    def blocks_of(half):
+        up = half[0:192].reshape(2, cols, rows)
+        down = half[192:384].reshape(2, cols, rows)
+        return up, down, half[384:432], half[432:].reshape(3, HALF, rows)
+
+    up0, down0, out0, near0 = blocks_of(first)
+    up1, down1, out1, near1 = blocks_of(second)
+    weight_grad = jnp.concatenate(
+        [
+            jnp.concatenate([near0, near1], axis=1),
+            jnp.concatenate([out0, out1], axis=0)[None],
+            up0,
+            up1,
+            down0,
+            down1,
+        ],
+        axis=0,
+    )
+    weight_grad = jnp.transpose(weight_grad, (2, 0, 1))
+    new_master, new_moment_one, new_moment_two = adam_step(
+        master, weight_grad * clip, moment_one, moment_two, rate_matrix, weight_decay
+    )
+    new_norm_params, new_norm_moment_one, new_norm_moment_two = adam_step(
+        norm_params, param_grad * clip, norm_moment_one, norm_moment_two, rate_vector, 0.0
+    )
+    return (
+        block_out,
+        patches_grad,
+        new_master,
+        new_master.astype(bf16),
+        new_moment_one,
+        new_moment_two,
+        new_norm_params,
+        new_norm_moment_one,
+        new_norm_moment_two,
+        grad_norm,
+    )
 
 
 def solution(mesh):
     tokens = P(("dp", "seq"), None)
     weights = P("dp", None, "seq")
+    small = mesh.shape["dp"] == 4 and mesh.shape["seq"] == 8
     return jax.shard_map(
-        local,
+        step_small if small else step_general,
         mesh=mesh,
         in_specs=(tokens, tokens, P("dp"), P(("dp", "seq")), weights, weights, weights, P(), P(), P()),
         out_specs=(tokens, tokens, weights, weights, weights, weights, P(), P(), P(), P()),

time: 656 us -> 406 us (0.62); the launches traced: 644 us -> 403 us
  local copies, waits for them, and re-layouts: 216 us -> 15.2 us
  matrix products: 134 us -> 0 us
  Pallas kernels: 0 us -> 126 us
  other arithmetic: 138 us -> 15.8 us
  waiting for transfers between devices: 89.4 us -> 155 us
  starting transfers between devices: 60 us -> 86.2 us
    pallas_call x0 -> x13, Pallas kernels: none -> 126 us  [call(): pl.pallas_call(body, name=name, out_shape=outs, in_specs=ins, out_specs=j...]
    dot_general x65 -> x0, matrix products: 115 us -> none  [the longest x20 25.8 us: mm(): return jnp.dot(a, b, preferred_element_type=f32)]
    ppermute x30 -> x54, waiting for transfers between devices: 41.4 us -> 126 us  [swap(): lax.ppermute(value, axis, [(i, i ^ bit) for i in range(lax.axis_size(axis...]
    convert_element_type x21 -> x15, other arithmetic: 45.9 us -> 4.93 us  [the longest x1 2.63 us: step_small(): new_master.astype(bf16)]
    another operation x30 -> x2, local copies, waits for them, and re-layouts: 38.8 us -> 1.01 us  [the longest x1 1 us: step_small(): near = jnp.stack([near, near_there], axis=1).reshape(8, 3 * HALF, 2 * rows)]
    unnamed x376 -> x139, local copies, waits for them, and re-layouts: 45.4 us -> 9.5 us
    ppermute x30 -> x54, starting transfers between devices: 19 us -> 53.8 us  [swap(): lax.ppermute(value, axis, [(i, i ^ bit) for i in range(lax.axis_size(axis...]
    another operation x33 -> x4, other arithmetic: 28.8 us -> 1.44 us  [the longest x1 0.66 us: step_small(): at = jnp.stack([x_place, y_place, core, place]).astype(jnp.int32)]
  transfers between devices with their start and end apart: 66 -> 72, of which waited for: 21 -> 36; matrix products, arithmetic and copies ran while one was open for 53% -> 4% of each run, Pallas kernels for 0% -> 16%
where the time goes in v2:
time: 406 us; the launch traced here: 403 us
  waiting for transfers between devices  155 us (38%)
  Pallas kernels  126 us (31%)
  starting transfers between devices  86.2 us (21%)
  other arithmetic  15.8 us (4%)
  local copies, waits for them, and re-layouts  15.2 us (4%)
  between operations  5.08 us (1%)
    pallas_call x13, Pallas kernels, call(): pl.pallas_call(body, name=name, out_shape=outs, in_specs=ins, out_specs=j...  126 us
    ppermute x54, waiting for transfers between devices, swap(): lax.ppermute(value, axis, [(i, i ^ bit) for i in range(lax.axis_size(axis...  126 us
    ppermute x54, starting transfers between devices, swap(): lax.ppermute(value, axis, [(i, i ^ bit) for i in range(lax.axis_size(axis...  53.8 us
    ppermute x18, starting transfers between devices, hop_quarter(): return lax.ppermute(value, 'seq', pairs)  32.4 us
    ppermute x18, waiting for transfers between devices, hop_quarter(): return lax.ppermute(value, 'seq', pairs)  29 us
    unnamed x139, local copies, waits for them, and re-layouts  9.5 us
  transfers between devices with their start and end apart: 72, of which 36 were waited for; matrix products, arithmetic and copies ran while one was open for 4% of the time, Pallas kernels for 16%

profile of v2, /device:TPU:0, one launch (start us, length us, event | category | flops | bytes accessed | tf_op | source)
XLA Modules:
  0.0 402.9 jit_solution(2507271530226428778)
XLA Ops:
  19.5 3.7 collective-permute-done.4
  28.0 12.7 %collective-permute-done.17.refs_11_ = bf16[432,384]{1,0:T(8,128)(2,1)S(1)} collective-permute-done((bf16[432,384]{1,0:T(8,128)(2,1)S(1)}, bf16[432,384]{1,0:T(8,128)(2,1)S(1)}, u32[]{:S(2)}, u32[]{:S(2)}) %collective-permute-start.17) | collective-permute-done | bytes 331808 | tf_op jit(solution)/shard_map/ppermute | solution.py:54
  44.9 6.8 %collective-permute-done.20.refs_5_ = bf16[432,384]{1,0:T(8,128)(2,1)S(1)} collective-permute-done((bf16[432,384]{1,0:T(8,128)(2,1)}, bf16[432,384]{1,0:T(8,128)(2,1)S(1)}, u32[]{:S(2)}, u32[]{:S(2)}) %collective-permute-start.20) | collective-permute-done | bytes 331808 | tf_op jit(solution)/shard_map/ppermute | solution.py:54
  53.0 5.9 %collective-permute-done.21.refs_7_ = bf16[432,384]{1,0:T(8,128)(2,1)S(1)} collective-permute-done((bf16[432,384]{1,0:T(8,128)(2,1)S(1)}, bf16[432,384]{1,0:T(8,128)(2,1)S(1)}, u32[]{:S(2)}, u32[]{:S(2)}) %collective-permute-start.21) | collective-permute-done | bytes 331808 | tf_op jit(solution)/shard_map/ppermute | solution.py:54
  63.9 5.4 %collective-permute-done.26.refs_4_ = bf16[432,384]{1,0:T(8,128)(2,1)S(1)} collective-permute-done((bf16[432,384]{1,0:T(8,128)(2,1)S(1)}, bf16[432,384]{1,0:T(8,128)(2,1)S(1)}, u32[]{:S(2)}, u32[]{:S(2)}) %collective-permute-start.26) | collective-permute-done | bytes 331808 | tf_op jit(solution)/shard_map/ppermute | solution.py:44
  77.5 5.5 %collective-permute-done.27.refs_6_ = bf16[432,384]{1,0:T(8,128)(2,1)S(1)} collective-permute-done((bf16[432,384]{1,0:T(8,128)(2,1)S(1)}, bf16[432,384]{1,0:T(8,128)(2,1)S(1)}, u32[]{:S(2)}, u32[]{:S(2)}) %collective-permute-start.27) | collective-permute-done | bytes 331808 | tf_op jit(solution)/shard_map/ppermute | solution.py:54
  83.0 5.5 %collective-permute-done.29.refs_7_ = bf16[432,384]{1,0:T(8,128)(2,1)S(1)} collective-permute-done((bf16[432,384]{1,0:T(8,128)(2,1)S(1)}, bf16[432,384]{1,0:T(8,128)(2,1)S(1)}, u32[]{:S(2)}, u32[]{:S(2)}) %collective-permute-start.29) | collective-permute-done | bytes 331808 | tf_op jit(solution)/shard_map/ppermute | solution.py:54
  98.4 3.6 collective-permute-done.7.b_ref
  102.0 4.2 %norm_project.5 = (bf16[512,768]{1,0:T(8,128)(2,1)}, bf16[512,768]{1,0:T(8,128)(2,1)}, bf16[3,256,128]{2,1,0:T(8,128)(2,1)}, bf16[3,512,128]{2,1,0:T(8,128)(2,1)}, bf16[3,512,128]{2,1,0:T(8,128)(2,1)}) custom-call(bf16[264,768]{1,0:T(8,128)(2,1)} %collective-permute-done.6.a_ref, bf16[264,768]{1,0:T(8,128)(2,1)} %collective-permute-done.7.b_ref, ...), custom_call_target="tpu_custom_call" | custom-call | tf_op jit(solution)/shard_map/norm_project/pallas_call | solution.py:361
  106.2 4.3 %norm_project.4 = (bf16[512,768]{1,0:T(8,128)(2,1)}, bf16[512,768]{1,0:T(8,128)(2,1)}, bf16[3,256,128]{2,1,0:T(8,128)(2,1)}, bf16[3,512,128]{2,1,0:T(8,128)(2,1)}, bf16[3,512,128]{2,1,0:T(8,128)(2,1)}) custom-call(bf16[264,768]{1,0:T(8,128)(2,1)} %copy-done.4, bf16[264,768]{1,0:T(8,128)(2,1)} %collective-permute-done.b_ref, ...), custom_call_target="tpu_custom_call" | custom-call | tf_op jit(solution)/shard_map/norm_project/pallas_call | solution.py:361
  110.6 4.3 %norm_project.6 = (bf16[512,768]{1,0:T(8,128)(2,1)}, bf16[512,768]{1,0:T(8,128)(2,1)}, bf16[3,256,128]{2,1,0:T(8,128)(2,1)}, bf16[3,512,128]{2,1,0:T(8,128)(2,1)}, bf16[3,512,128]{2,1,0:T(8,128)(2,1)}) custom-call(bf16[264,768]{1,0:T(8,128)(2,1)} %collective-permute-done.8.a_ref, bf16[264,768]{1,0:T(8,128)(2,1)} %collective-permute-done.9.b_ref, ...), custom_call_target="tpu_custom_call" | custom-call | tf_op jit(solution)/shard_map/norm_project/pallas_call | solution.py:361
  114.9 3.3 collective-permute-done.11.b_ref
  118.9 4.2 %norm_project.7 = (bf16[512,768]{1,0:T(8,128)(2,1)}, bf16[512,768]{1,0:T(8,128)(2,1)}, bf16[3,256,128]{2,1,0:T(8,128)(2,1)}, bf16[3,512,128]{2,1,0:T(8,128)(2,1)}, bf16[3,512,128]{2,1,0:T(8,128)(2,1)}) custom-call(bf16[264,768]{1,0:T(8,128)(2,1)} %collective-permute-done.10.a_ref, bf16[264,768]{1,0:T(8,128)(2,1)} %copy-done.37, ...), custom_call_target="tpu_custom_call" | custom-call | tf_op jit(solution)/shard_map/norm_project/pallas_call | solution.py:361
  123.2 36.5 %attend.1 = (bf16[256,192]{1,0:T(8,128)(2,1)}, bf16[256,192]{1,0:T(8,128)(2,1)}, bf16[256,192]{1,0:T(8,128)(2,1)}, bf16[256,192]{1,0:T(8,128)(2,1)}, f32[3,4,256...) custom-call(s32[16]{0:T(128)} %reshape.140.seen_ref, ...), custom_call_target="tpu_custom_call" | custom-call | tf_op jit(solution)/shard_map/attend/pallas_call | solution.py:361
  164.2 3.2 place_out.1.w_ref
  169.7 4.1 %collective-permute-done.14.m3 = bf16[256,192]{1,0:T(8,128)(2,1)S(1)} collective-permute-done((bf16[256,192]{1,0:T(8,128)(2,1)}, bf16[256,192]{1,0:T(8,128)(2,1)S(1)}, u32[]{:S(2)}, u32[]{:S(2)}) %collective-permute-start.14) | collective-permute-done | bytes 98336 | tf_op jit(solution)/shard_map/ppermute | solution.py:44
  174.5 3.7 out_norm.1
  180.8 9.5 %mlp.2 = (f32[512,768]{1,0:T(8,128)}, f32[512,768]{1,0:T(8,128)}, bf16[2,384,384]{2,1,0:T(8,128)(2,1)}, bf16[2,384,384]{2,1,0:T(8,128)(2,1)}, bf16[2,384,384]{2,...) custom-call(s32[4]{0:T(128)} %pad_add_fusion.at_ref, bf16[256,768]{1,0:T(8,128)(2,1)} %get-tuple-element.106.refs_0_, ...), custom_call_target="tpu_custom_call" | custom-call | tf_op jit(solution)/shard_map/mlp/pallas_call | solution.py:361
  190.3 10.5 %mlp.3 = (f32[256,768]{1,0:T(8,128)}, f32[256,768]{1,0:T(8,128)}, bf16[2,384,384]{2,1,0:T(8,128)(2,1)}, bf16[2,384,384]{2,1,0:T(8,128)(2,1)}, bf16[2,384,384]{2,...) custom-call(s32[4]{0:T(128)} %pad_add_fusion.at_ref, ...), custom_call_target="tpu_custom_call" | custom-call | tf_op jit(solution)/shard_map/mlp/pallas_call | solution.py:361
  203.6 5.6 %norm_out_back.1 = (f32[256,768]{1,0:T(8,128)}, f32[8,768]{1,0:T(8,128)}, bf16[256,192]{1,0:T(8,128)(2,1)}, bf16[256,192]{1,0:T(8,128)(2,1)}, bf16[256,192]{1,0:...) custom-call(s32[4]{0:T(128)} %pad_add_fusion.at_ref, ...), custom_call_target="tpu_custom_call" | custom-call | tf_op jit(solution)/shard_map/norm_out_back/pallas_call | solution.py:361
  213.4 9.0 %collective-permute-done.35.refs_14_ = bf16[256,192]{1,0:T(8,128)(2,1)S(1)} collective-permute-done((bf16[256,192]{1,0:T(8,128)(2,1)}, bf16[256,192]{1,0:T(8,128)(2,1)S(1)}, u32[]{:S(2)}, u32[]{:S(2)}) %collective-permute-start.35) | collective-permute-done | bytes 98336 | tf_op jit(solution)/shard_map/ppermute | solution.py:44
  223.1 26.9 %attend_back.1 = (bf16[256,192]{1,0:T(8,128)(2,1)}, bf16[256,192]{1,0:T(8,128)(2,1)}, bf16[256,192]{1,0:T(8,128)(2,1)}, bf16[256,192]{1,0:T(8,128)(2,1)}, bf16[5...) custom-call(s32[16]{0:T(128)} %reshape.140.seen_ref, ...), custom_call_target="tpu_custom_call" | custom-call | tf_op jit(solution)/shard_map/attend_back/pallas_call | solution.py:361
  250.0 10.0 %project_back.1 = (bf16[256,768]{1,0:T(8,128)(2,1)}, bf16[256,768]{1,0:T(8,128)(2,1)}, bf16[256,768]{1,0:T(8,128)(2,1)}, bf16[256,768]{1,0:T(8,128)(2,1)}, bf16[...) custom-call(s32[4]{0:T(128)} %pad_add_fusion.at_ref, ...), custom_call_target="tpu_custom_call" | custom-call | tf_op jit(solution)/shard_map/project_back/pallas_call | solution.py:361
  265.6 12.2 %collective-permute-done.68 = f32[4,768]{1,0:T(4,128)S(1)} collective-permute-done((f32[4,768]{1,0:T(4,128)S(1)}, f32[4,768]{1,0:T(4,128)S(1)}, u32[]{:S(2)}, u32[]{:S(2)}) %collective-permute-start.68) | collective-permute-done | bytes 12320 | tf_op jit(solution)/shard_map/ppermute | solution.py:54
  292.1 11.0 %collective-permute-done.50 = bf16[2,384,384]{2,1,0:T(8,128)(2,1)S(1)} collective-permute-done((bf16[2,384,384]{2,1,0:T(8,128)(2,1)}, bf16[2,384,384]{2,1,0:T(8,128)(2,1)S(1)}, u32[]{:S(2)}, u32[]{:S(2)}) %collective-permute-start.50) | collective-permute-done | bytes 589856 | tf_op jit(solution)/shard_map/ppermute | solution.py:54
  304.9 10.4 %collective-permute-done.45 = bf16[2,384,384]{2,1,0:T(8,128)(2,1)S(1)} collective-permute-done((bf16[2,384,384]{2,1,0:T(8,128)(2,1)}, bf16[2,384,384]{2,1,0:T(8,128)(2,1)S(1)}, u32[]{:S(2)}, u32[]{:S(2)}) %collective-permute-start.45) | collective-permute-done | bytes 589856 | tf_op jit(solution)/shard_map/ppermute | solution.py:54
  321.6 4.0 collective-permute-done.47
  328.1 5.9 %collective-permute-done.48 = bf16[432,384]{1,0:T(8,128)(2,1)S(1)} collective-permute-done((bf16[432,384]{1,0:T(8,128)(2,1)S(1)}, bf16[432,384]{1,0:T(8,128)(2,1)S(1)}, u32[]{:S(2)}, u32[]{:S(2)}) %collective-permute-start.48) | collective-permute-done | bytes 331808 | tf_op jit(solution)/shard_map/ppermute | solution.py:54
  337.5 4.5 %collective-permute-done.51 = bf16[432,384]{1,0:T(8,128)(2,1)S(1)} collective-permute-done((bf16[432,384]{1,0:T(8,128)(2,1)S(1)}, bf16[432,384]{1,0:T(8,128)(2,1)S(1)}, u32[]{:S(2)}, u32[]{:S(2)}) %collective-permute-start.51) | collective-permute-done | bytes 331808 | tf_op jit(solution)/shard_map/ppermute | solution.py:54
  347.6 5.1 %collective-permute-done.54 = bf16[432,384]{1,0:T(8,128)(2,1)S(1)} collective-permute-done((bf16[432,384]{1,0:T(8,128)(2,1)S(1)}, bf16[432,384]{1,0:T(8,128)(2,1)S(1)}, u32[]{:S(2)}, u32[]{:S(2)}) %collective-permute-start.54) | collective-permute-done | bytes 331808 | tf_op jit(solution)/shard_map/ppermute | solution.py:54
  356.0 6.8 %collective-permute-done.60 = bf16[3,48,384]{2,1,0:T(8,128)(2,1)S(1)} collective-permute-done((bf16[3,48,384]{2,1,0:T(8,128)(2,1)S(1)}, bf16[3,48,384]{2,1,0:T(8,128)(2,1)S(1)}, u32[]{:S(2)}, u32[]{:S(2)}) %collective-permute-start.60) | collective-permute-done | bytes 110624 | tf_op jit(solution)/shard_map/ppermute | solution.py:54
  367.4 6.2 %collective-permute-done.55 = bf16[432,384]{1,0:T(8,128)(2,1)S(1)} collective-permute-done((bf16[432,384]{1,0:T(8,128)(2,1)S(1)}, bf16[432,384]{1,0:T(8,128)(2,1)S(1)}, u32[]{:S(2)}, u32[]{:S(2)}) %collective-permute-start.55) | collective-permute-done | bytes 331808 | tf_op jit(solution)/shard_map/ppermute | solution.py:44
  (356 shorter events, 143.5 us)
Async XLA Ops:
  3.2 14.4 %collective-permute-start.6 = (bf16[264,768]{1,0:T(8,128)(2,1)S(1)}, bf16[264,768]{1,0:T(8,128)(2,1)}, u32[]{:S(2)}, u32[]{:S(2)}) collective-permute-start(bf16[264,768]{1,0:T(8,128)(2,1)S(1)} %fusion.17.a_ref), channel_id=1, source_target_pairs={{0,2},{1,3},{2,6},{3,7},{6,4},{7,5},{4,0},{5,1},{8,10},{9,11},{10,... | collective-permute-start | bytes 1216520 | tf_op jit(solution)/shard_map/ppermute | solution.py:44
  9.8 15.3 %collective-permute-start.18 = (bf16[432,384]{1,0:T(8,128)(2,1)S(1)}, bf16[432,384]{1,0:T(8,128)(2,1)}, u32[]{:S(2)}, u32[]{:S(2)}) collective-permute-start(bf16[432,384]{1,0:T(8,128)(2,1)S(1)} %pad_maximum_fusion.3.refs_8_), channel_id=1, source_target_pairs={{0,2},{1,3},{2,6},{3,7},{6,4},{7,5},{4,0},{5,1},{8,10},{9,11},{10,... | collective-permute-start | bytes 995336 | tf_op jit(solution)/shard_map/ppermute | solution.py:44
  12.5 14.0 %collective-permute-start.15 = (bf16[432,384]{1,0:T(8,128)(2,1)S(1)}, bf16[432,384]{1,0:T(8,128)(2,1)S(1)}, u32[]{:S(2)}, u32[]{:S(2)}) collective-permute-start(bf16[432,384]{1,0:T(8,128)(2,1)S(1)} %pad_maximum_fusion.3.refs_8_), channel_id=1, source_target_pairs={{0,16},{8,24},{16,0},{24,8},{1,17},{9,25},{17,1},{25,9},{2,18},{10... | collective-permute-start | bytes 995336 | tf_op jit(solution)/shard_map/ppermute | solution.py:54
  13.0 14.5 %collective-permute-start.16 = (bf16[432,384]{1,0:T(8,128)(2,1)S(1)}, bf16[432,384]{1,0:T(8,128)(2,1)S(1)}, u32[]{:S(2)}, u32[]{:S(2)}) collective-permute-start(bf16[432,384]{1,0:T(8,128)(2,1)S(1)} %pad_maximum_fusion.3.refs_8_), channel_id=1, source_target_pairs={{0,1},{1,0},{2,3},{3,2},{4,5},{5,4},{6,7},{7,6},{8,9},{9,8},{10,11... | collective-permute-start | bytes 995336 | tf_op jit(solution)/shard_map/ppermute | solution.py:54
  17.7 88.5 %collective-permute-start = (bf16[264,768]{1,0:T(8,128)(2,1)S(1)}, bf16[264,768]{1,0:T(8,128)(2,1)}, u32[]{:S(2)}, u32[]{:S(2)}) collective-permute-start(bf16[264,768]{1,0:T(8,128)(2,1)S(1)} %fusion.17.a_ref), channel_id=1, source_target_pairs={{0,1},{1,0},{2,3},{3,2},{4,5},{5,4},{6,7},{7,6},{8,9},{9,8},{10,11... | collective-permute-start | bytes 1216520 | tf_op jit(solution)/shard_map/ppermute | solution.py:54
  23.2 36.8 %collective-permute-start.8 = (bf16[264,768]{1,0:T(8,128)(2,1)}, bf16[264,768]{1,0:T(8,128)(2,1)}, u32[]{:S(2)}, u32[]{:S(2)}) collective-permute-start(bf16[264,768]{1,0:T(8,128)(2,1)} %collective-permute-done.6.a_ref), channel_id=1, source_target_pairs={{0,2},{1,3},{2,6},{3,7},{6,4},{7,5},{4,0},{5,1},{8,10},{9,11},{10,... | collective-permute-start | bytes 1216520 | tf_op jit(solution)/shard_map/ppermute | solution.py:44
  25.1 18.7 %collective-permute-start.19 = (bf16[432,384]{1,0:T(8,128)(2,1)}, bf16[432,384]{1,0:T(8,128)(2,1)S(1)}, u32[]{:S(2)}, u32[]{:S(2)}) collective-permute-start(bf16[432,384]{1,0:T(8,128)(2,1)} %collective-permute-done.18.refs_4_), channel_id=1, source_target_pairs={{0,16},{8,24},{16,0},{24,8},{1,17},{9,25},{17,1},{25,9},{2,18},{10... | collective-permute-start | bytes 995336 | tf_op jit(solution)/shard_map/ppermute | solution.py:54
  26.4 15.0 %collective-permute-start.22 = (bf16[432,384]{1,0:T(8,128)(2,1)}, bf16[432,384]{1,0:T(8,128)(2,1)S(1)}, u32[]{:S(2)}, u32[]{:S(2)}) collective-permute-start(bf16[432,384]{1,0:T(8,128)(2,1)} %collective-permute-done.18.refs_4_), channel_id=1, source_target_pairs={{0,2},{1,3},{2,6},{3,7},{6,4},{7,5},{4,0},{5,1},{8,10},{9,11},{10,... | collective-permute-start | bytes 995336 | tf_op jit(solution)/shard_map/ppermute | solution.py:44
  27.5 13.3 %collective-permute-start.17 = (bf16[432,384]{1,0:T(8,128)(2,1)S(1)}, bf16[432,384]{1,0:T(8,128)(2,1)S(1)}, u32[]{:S(2)}, u32[]{:S(2)}) collective-permute-start(bf16[432,384]{1,0:T(8,128)(2,1)S(1)} %collective-permute-done.16.refs_9_), channel_id=1, source_target_pairs={{0,16},{8,24},{16,0},{24,8},{1,17},{9,25},{17,1},{25,9},{2,18},{10... | collective-permute-start | bytes 995336 | tf_op jit(solution)/shard_map/ppermute | solution.py:54
  41.5 18.7 %collective-permute-start.23 = (bf16[432,384]{1,0:T(8,128)(2,1)S(1)}, bf16[432,384]{1,0:T(8,128)(2,1)S(1)}, u32[]{:S(2)}, u32[]{:S(2)}) collective-permute-start(bf16[432,384]{1,0:T(8,128)(2,1)S(1)} %collective-permute-done.22.refs_8_), channel_id=1, source_target_pairs={{0,16},{8,24},{16,0},{24,8},{1,17},{9,25},{17,1},{25,9},{2,18},{10... | collective-permute-start | bytes 995336 | tf_op jit(solution)/shard_map/ppermute | solution.py:54
  43.8 18.6 %collective-permute-start.24 = (bf16[432,384]{1,0:T(8,128)(2,1)S(1)}, bf16[432,384]{1,0:T(8,128)(2,1)S(1)}, u32[]{:S(2)}, u32[]{:S(2)}) collective-permute-start(bf16[432,384]{1,0:T(8,128)(2,1)S(1)} %collective-permute-done.22.refs_8_), channel_id=1, source_target_pairs={{0,1},{1,0},{2,3},{3,2},{4,5},{5,4},{6,7},{7,6},{8,9},{9,8},{10,11... | collective-permute-start | bytes 995336 | tf_op jit(solution)/shard_map/ppermute | solution.py:54
  60.1 30.8 %collective-permute-start.5 = (bf16[4,144,384]{2,1,0:T(8,128)(2,1)S(1)}, bf16[4,144,384]{2,1,0:T(8,128)(2,1)S(1)}, u32[]{:S(2)}, u32[]{:S(2)}) collective-permute-start(bf16[4,144,384]{2,1,0:T(8,128)(2,1)S(1)} %get-tuple-element.206), channel_id=1, source_target_pairs={{0,8},{8,0},{16,24},{24,16},{1,9},{9,1},{17,25},{25,17},{2,10},{10... | collective-permute-start | bytes 1327112 | tf_op jit(solution)/shard_map/ppermute | solution.py:54
  60.2 31.3 %collective-permute-start.10 = (bf16[264,768]{1,0:T(8,128)(2,1)}, bf16[264,768]{1,0:T(8,128)(2,1)}, u32[]{:S(2)}, u32[]{:S(2)}) collective-permute-start(bf16[264,768]{1,0:T(8,128)(2,1)} %collective-permute-done.8.a_ref), channel_id=1, source_target_pairs={{0,2},{1,3},{2,6},{3,7},{6,4},{7,5},{4,0},{5,1},{8,10},{9,11},{10,... | collective-permute-start | bytes 1216520 | tf_op jit(solution)/shard_map/ppermute | solution.py:44
  88.6 74.8 %collective-permute-start.30 = (bf16[16,48,384]{2,1,0:T(8,128)(2,1)S(1)}, bf16[16,48,384]{2,1,0:T(8,128)(2,1)S(1)}, u32[]{:S(2)}, u32[]{:S(2)}) collective-permute-start(bf16[16,48,384]{2,1,0:T(8,128)(2,1)S(1)} %constant_dynamic-update-slice_fusion.own_ref), channel_id=1, source_target_pairs={{0,8},{8,0},{16,24},{24,16},{1,9},{9,1},{17,25},{25,17},{2,10},{10... | collective-permute-start | bytes 1769480 | tf_op jit(solution)/shard_map/ppermute | solution.py:54
  90.9 19.8 %collective-permute-start.9 = (bf16[264,768]{1,0:T(8,128)(2,1)}, bf16[264,768]{1,0:T(8,128)(2,1)}, u32[]{:S(2)}, u32[]{:S(2)}) collective-permute-start(bf16[264,768]{1,0:T(8,128)(2,1)} %collective-permute-done.8.a_ref), channel_id=1, source_target_pairs={{0,1},{1,0},{2,3},{3,2},{4,5},{5,4},{6,7},{7,6},{8,9},{9,8},{10,11... | collective-permute-start | bytes 1216520 | tf_op jit(solution)/shard_map/ppermute | solution.py:54
  91.4 26.8 %collective-permute-start.11 = (bf16[264,768]{1,0:T(8,128)(2,1)}, bf16[264,768]{1,0:T(8,128)(2,1)S(1)}, u32[]{:S(2)}, u32[]{:S(2)}) collective-permute-start(bf16[264,768]{1,0:T(8,128)(2,1)} %collective-permute-done.10.a_ref), channel_id=1, source_target_pairs={{0,1},{1,0},{2,3},{3,2},{4,5},{5,4},{6,7},{7,6},{8,9},{9,8},{10,11... | collective-permute-start | bytes 1216520 | tf_op jit(solution)/shard_map/ppermute | solution.py:54
  102.0 76.2 %collective-permute-start.32 = (bf16[256,768]{1,0:T(8,128)(2,1)S(1)}, bf16[256,768]{1,0:T(8,128)(2,1)S(1)}, u32[]{:S(2)}, u32[]{:S(2)}) collective-permute-start(bf16[256,768]{1,0:T(8,128)(2,1)S(1)} %copy-done.3), channel_id=1, source_target_pairs={{0,8},{8,0},{16,24},{24,16},{1,9},{9,1},{17,25},{25,17},{2,10},{10... | collective-permute-start | bytes 1179656 | tf_op jit(solution)/shard_map/ppermute | solution.py:54
  261.1 27.8 %collective-permute-start.56 = (bf16[2,384,384]{2,1,0:T(8,128)(2,1)}, bf16[2,384,384]{2,1,0:T(8,128)(2,1)S(1)}, u32[]{:S(2)}, u32[]{:S(2)}) collective-permute-start(bf16[2,384,384]{2,1,0:T(8,128)(2,1)} %get-tuple-element.163), channel_id=1, source_target_pairs={{0,16},{8,24},{16,0},{24,8},{1,17},{9,25},{17,1},{25,9},{2,18},{10... | collective-permute-start | bytes 1769480 | tf_op jit(solution)/shard_map/ppermute | solution.py:54
  262.7 21.9 %collective-permute-start.33 = (bf16[256,768]{1,0:T(8,128)(2,1)}, bf16[256,768]{1,0:T(8,128)(2,1)S(1)}, u32[]{:S(2)}, u32[]{:S(2)}) collective-permute-start(bf16[256,768]{1,0:T(8,128)(2,1)} %get-tuple-element.110), channel_id=1, source_target_pairs={{0,8},{8,0},{16,24},{24,16},{1,9},{9,1},{17,25},{25,17},{2,10},{10... | collective-permute-start | bytes 1179656 | tf_op jit(solution)/shard_map/ppermute | solution.py:54
  262.9 14.8 %collective-permute-start.68 = (f32[4,768]{1,0:T(4,128)S(1)}, f32[4,768]{1,0:T(4,128)S(1)}, u32[]{:S(2)}, u32[]{:S(2)}) collective-permute-start(f32[4,768]{1,0:T(4,128)S(1)} %fusion.19), channel_id=1, source_target_pairs={{0,16},{8,24},{16,0},{24,8},{1,17},{9,25},{17,1},{25,9},{2,18},{10... | collective-permute-start | bytes 36872 | tf_op jit(solution)/shard_map/ppermute | solution.py:54
  264.2 26.2 %collective-permute-start.53 = (bf16[2,384,384]{2,1,0:T(8,128)(2,1)}, bf16[2,384,384]{2,1,0:T(8,128)(2,1)S(1)}, u32[]{:S(2)}, u32[]{:S(2)}) collective-permute-start(bf16[2,384,384]{2,1,0:T(8,128)(2,1)} %get-tuple-element.161), channel_id=1, source_target_pairs={{0,16},{8,24},{16,0},{24,8},{1,17},{9,25},{17,1},{25,9},{2,18},{10... | collective-permute-start | bytes 1769480 | tf_op jit(solution)/shard_map/ppermute | solution.py:54
  279.9 23.2 %collective-permute-start.50 = (bf16[2,384,384]{2,1,0:T(8,128)(2,1)}, bf16[2,384,384]{2,1,0:T(8,128)(2,1)S(1)}, u32[]{:S(2)}, u32[]{:S(2)}) collective-permute-start(bf16[2,384,384]{2,1,0:T(8,128)(2,1)} %get-tuple-element.159), channel_id=1, source_target_pairs={{0,16},{8,24},{16,0},{24,8},{1,17},{9,25},{17,1},{25,9},{2,18},{10... | collective-permute-start | bytes 1769480 | tf_op jit(solution)/shard_map/ppermute | solution.py:54
  282.4 32.9 %collective-permute-start.45 = (bf16[2,384,384]{2,1,0:T(8,128)(2,1)}, bf16[2,384,384]{2,1,0:T(8,128)(2,1)S(1)}, u32[]{:S(2)}, u32[]{:S(2)}) collective-permute-start(bf16[2,384,384]{2,1,0:T(8,128)(2,1)} %get-tuple-element.155), channel_id=1, source_target_pairs={{0,16},{8,24},{16,0},{24,8},{1,17},{9,25},{17,1},{25,9},{2,18},{10... | collective-permute-start | bytes 1769480 | tf_op jit(solution)/shard_map/ppermute | solution.py:54
  288.9 28.0 %collective-permute-start.46 = (bf16[8,48,768]{2,1,0:T(8,128)(2,1)S(1)}, bf16[8,48,768]{2,1,0:T(8,128)(2,1)S(1)}, u32[]{:S(2)}, u32[]{:S(2)}) collective-permute-start(bf16[8,48,768]{2,1,0:T(8,128)(2,1)S(1)} %copy-done.53), channel_id=1, source_target_pairs={{0,8},{8,0},{16,24},{24,16},{1,9},{9,1},{17,25},{25,17},{2,10},{10... | collective-permute-start | bytes 1769480 | tf_op jit(solution)/shard_map/ppermute | solution.py:54
  289.0 37.4 %collective-permute-start.58 = (bf16[6,48,768]{2,1,0:T(8,128)(2,1)S(1)}, bf16[6,48,768]{2,1,0:T(8,128)(2,1)S(1)}, u32[]{:S(2)}, u32[]{:S(2)}) collective-permute-start(bf16[6,48,768]{2,1,0:T(8,128)(2,1)S(1)} %copy-done.54), channel_id=1, source_target_pairs={{0,8},{8,0},{16,24},{24,16},{1,9},{9,1},{17,25},{25,17},{2,10},{10... | collective-permute-start | bytes 1327112 | tf_op jit(solution)/shard_map/ppermute | solution.py:54
  290.4 28.4 %collective-permute-start.38 = (bf16[256,768]{1,0:T(8,128)(2,1)S(1)}, bf16[256,768]{1,0:T(8,128)(2,1)S(1)}, u32[]{:S(2)}, u32[]{:S(2)}) collective-permute-start(bf16[256,768]{1,0:T(8,128)(2,1)S(1)} %copy-done.58), channel_id=1, source_target_pairs={{0,1},{1,0},{2,3},{3,2},{4,5},{5,4},{6,7},{7,6},{8,9},{9,8},{10,11... | collective-permute-start | bytes 1179656 | tf_op jit(solution)/shard_map/ppermute | solution.py:54
  303.0 42.3 %collective-permute-start.40 = (bf16[256,768]{1,0:T(8,128)(2,1)S(1)}, bf16[256,768]{1,0:T(8,128)(2,1)S(1)}, u32[]{:S(2)}, u32[]{:S(2)}) collective-permute-start(bf16[256,768]{1,0:T(8,128)(2,1)S(1)} %copy-done.57), channel_id=1, source_target_pairs={{0,1},{1,0},{2,3},{3,2},{4,5},{5,4},{6,7},{7,6},{8,9},{9,8},{10,11... | collective-permute-start | bytes 1179656 | tf_op jit(solution)/shard_map/ppermute | solution.py:54
  315.3 50.1 %collective-permute-start.42 = (bf16[256,768]{1,0:T(8,128)(2,1)S(1)}, bf16[256,768]{1,0:T(8,128)(2,1)S(1)}, u32[]{:S(2)}, u32[]{:S(2)}) collective-permute-start(bf16[256,768]{1,0:T(8,128)(2,1)S(1)} %copy-done.56), channel_id=1, source_target_pairs={{0,1},{1,0},{2,3},{3,2},{4,5},{5,4},{6,7},{7,6},{8,9},{9,8},{10,11... | collective-permute-start | bytes 1179656 | tf_op jit(solution)/shard_map/ppermute | solution.py:54
  319.0 27.9 %collective-permute-start.39 = (bf16[256,768]{1,0:T(8,128)(2,1)S(1)}, bf16[256,768]{1,0:T(8,128)(2,1)S(1)}, u32[]{:S(2)}, u32[]{:S(2)}) collective-permute-start(bf16[256,768]{1,0:T(8,128)(2,1)S(1)} %add_convert_fusion.11), channel_id=1, source_target_pairs={{0,2},{1,3},{2,6},{3,7},{6,4},{7,5},{4,0},{5,1},{8,10},{9,11},{10,... | collective-permute-start | bytes 1179656 | tf_op jit(solution)/shard_map/ppermute | solution.py:44
  345.4 33.3 %collective-permute-start.44 = (bf16[256,768]{1,0:T(8,128)(2,1)S(1)}, bf16[256,768]{1,0:T(8,128)(2,1)S(1)}, u32[]{:S(2)}, u32[]{:S(2)}) collective-permute-start(bf16[256,768]{1,0:T(8,128)(2,1)S(1)} %copy-done.55), channel_id=1, source_target_pairs={{0,1},{1,0},{2,3},{3,2},{4,5},{5,4},{6,7},{7,6},{8,9},{9,8},{10,11... | collective-permute-start | bytes 1179656 | tf_op jit(solution)/shard_map/ppermute | solution.py:54
  346.9 15.9 %collective-permute-start.60 = (bf16[3,48,384]{2,1,0:T(8,128)(2,1)S(1)}, bf16[3,48,384]{2,1,0:T(8,128)(2,1)S(1)}, u32[]{:S(2)}, u32[]{:S(2)}) collective-permute-start(bf16[3,48,384]{2,1,0:T(8,128)(2,1)S(1)} %slice.273), channel_id=1, source_target_pairs={{0,1},{1,0},{2,3},{3,2},{4,5},{5,4},{6,7},{7,6},{8,9},{9,8},{10,11... | collective-permute-start | bytes 331784 | tf_op jit(solution)/shard_map/ppermute | solution.py:54
  352.7 14.7 %collective-permute-start.57 = (bf16[432,384]{1,0:T(8,128)(2,1)S(1)}, bf16[432,384]{1,0:T(8,128)(2,1)S(1)}, u32[]{:S(2)}, u32[]{:S(2)}) collective-permute-start(bf16[432,384]{1,0:T(8,128)(2,1)S(1)} %pad_maximum_fusion.7), channel_id=1, source_target_pairs={{0,1},{1,0},{2,3},{3,2},{4,5},{5,4},{6,7},{7,6},{8,9},{9,8},{10,11... | collective-permute-start | bytes 995336 | tf_op jit(solution)/shard_map/ppermute | solution.py:54
  (100 other events, 1089.6 us)
